TPU v7x, 768 devices: a whole 4x8x12 slice. The times are simulated.
768 devices in a mesh: dp: 8 (over y_hi, x), zero: 96 (over z, y_lo, core).
Axes of the slice: x: 4, y: 8 (y_hi: 2, y_lo: 4; y = y_hi * 4 + y_lo), z: 12, core: 2. Of those that a mesh axis runs over, the one named last changes fastest.
Arguments:
- feats: bfloat16 [98304, 6144], P(('dp', 'zero')), may hold values from -6 to 6
- short_filter: bfloat16 [7, 6144], P(None, 'zero'), may hold values from -2 to 2
- medium_filter: float32 [128, 128], replicated, may hold values from -0.5 to 0.5
- doc_ids: int32 [768, 128], P(('dp', 'zero')), may hold values from 0 to 2, never falling along the last dimension, each value on 1 to 112 neighbouring positions
- counts: int32 [768], P(('dp', 'zero')), may hold values from 64 to 128
- plan: int32 [768], P(('dp', 'zero')), may hold values from 0 to 7, as said below
- cotangent: bfloat16 [98304, 2048], P(('dp', 'zero')), may hold values from -6 to 6
Outputs:
- mixed: bfloat16 [98304, 2048], P(('dp', 'zero'))
- feats_grad: bfloat16 [98304, 6144], P(('dp', 'zero'))
- short_grad: float32 [7, 6144], P(None, 'zero')
- medium_grad: float32 [128, 128], replicated
Inputs may be any that keep to these rules, and one draw needn't show every extreme that they name: `plan`: every data rank is named by some tile.
All inputs are finite; a program needn't handle non-finite values.
Results may differ from a plain program's by a relative error of at most 0.0058.
Values may be sent and summed in bfloat16 or wider, within the bound.
No kernel may reach another device: no remote copies, remote signals or barrier semaphores. Data moves between devices by JAX's collectives and lax.ppermute only.
A program may use at most 64 MiB of HBM per device.

v0:
```python
import jax
import jax.numpy as jnp
from jax import lax
from jax.sharding import PartitionSpec as P

SHORT = 7


def shift_down(values, offset):
    return jnp.concatenate(
        [jnp.zeros((offset, values.shape[1]), values.dtype), values[: values.shape[0] - offset]], 0
    )


def shift_up(values, offset):
    return jnp.concatenate([values[offset:], jnp.zeros((offset, values.shape[1]), values.dtype)], 0)


def short_masks(segment, length):
    masks = []
    for offset in range(SHORT):
        earlier = jnp.concatenate([jnp.full((offset,), -1, jnp.int32), segment[: length - offset]])
        masks.append((earlier == segment).astype(jnp.float32)[:, None])
    return masks


def shards(feats, short_filter, medium_filter, doc_ids, counts, plan, cotangent):
    replicas = lax.axis_size("dp")
    zeros_count = lax.axis_size("zero")
    tile_count = replicas * zeros_count
    length = feats.shape[0]
    width = cotangent.shape[1]
    member = (plan[0] == jnp.arange(replicas)).astype(jnp.float32)
    totals = lax.psum(member * counts[0].astype(jnp.float32), ("dp", "zero"))
    weighting = length * tile_count / (replicas * jnp.sum(member * totals))
    gathered = lax.all_gather(short_filter, "zero", axis=1, tiled=True)
    segment = doc_ids[0]
    masks = short_masks(segment, length)
    position = jnp.arange(length)
    living = (position < counts[0]).astype(jnp.float32)[:, None]
    convolved = jnp.zeros(feats.shape, jnp.float32)
    for offset in range(SHORT):
        convolved = (
            convolved
            + gathered[offset].astype(jnp.float32)
            * shift_down(feats, offset).astype(jnp.float32)
            * masks[offset]
        )
    query_part = convolved[:, :width]
    key_part = convolved[:, width : 2 * width]
    value_part = convolved[:, 2 * width :]
    product = (key_part * value_part).astype(jnp.bfloat16)
    groups = medium_filter.shape[1]
    taps_count = medium_filter.shape[0]
    gsize_here = width // groups
    product_cols = product.reshape(length, groups, gsize_here).transpose(1, 2, 0)
    lag_index = jnp.arange(taps_count)[:, None, None]
    later = position[None, :, None]
    earlier = position[None, None, :]
    same_doc = (segment[:, None] == segment[None, :])[None]
    selector = (
        ((later - earlier == lag_index) & same_doc)
        .astype(jnp.bfloat16)
        .reshape(taps_count, length * length)
    )
    taps_rows = medium_filter.astype(jnp.bfloat16).T
    toeplitz = jnp.dot(taps_rows, selector, preferred_element_type=jnp.float32).astype(jnp.bfloat16)
    toeplitz = toeplitz.reshape(groups, length, length)
    long_cols = jnp.einsum(
        "gts,gcs->gct", toeplitz, product_cols, preferred_element_type=jnp.float32
    )
    long_conv = long_cols.transpose(2, 0, 1).reshape(length, width)
    mixed = (living * query_part * long_conv).astype(jnp.bfloat16)
    grad_out = cotangent.astype(jnp.float32) * living * weighting
    grad_query = grad_out * long_conv
    grad_long = (grad_out * query_part).astype(jnp.bfloat16)
    grad_cols = grad_long.reshape(length, groups, gsize_here).transpose(1, 2, 0)
    grad_prod_cols = jnp.einsum(
        "gts,gct->gcs", toeplitz, grad_cols, preferred_element_type=jnp.float32
    )
    grad_product = grad_prod_cols.transpose(2, 0, 1).reshape(length, width)
    crossed = jnp.einsum(
        "gct,gcs->gts", grad_cols, product_cols, preferred_element_type=jnp.float32
    )
    crossed = crossed.reshape(groups, length * length)
    medium_part = lax.dot_general(
        crossed,
        selector.astype(jnp.float32),
        (((1,), (1,)), ((), ())),
        precision=lax.Precision.HIGHEST,
    ).T
    grad_short = jnp.concatenate(
        [grad_query, grad_product * value_part, grad_product * key_part], 1
    )
    grad_feats = jnp.zeros(feats.shape, jnp.float32)
    short_rows = []
    for offset in range(SHORT):
        masked = grad_short * masks[offset]
        grad_feats = grad_feats + gathered[offset].astype(jnp.float32) * shift_up(masked, offset)
        short_rows.append(jnp.sum(masked * shift_down(feats, offset).astype(jnp.float32), 0))
    short_local = jnp.stack(short_rows)
    medium_grad = lax.psum(medium_part, ("dp", "zero"))
    zero_share = lax.psum_scatter(short_local, "zero", scatter_dimension=1, tiled=True)
    short_grad = lax.psum(zero_share, "dp")
    return (mixed, grad_feats.astype(jnp.bfloat16), short_grad, medium_grad)


def solution(mesh):
    in_specs = (
        P(("dp", "zero"), None),
        P(None, "zero"),
        P(),
        P(("dp", "zero"), None),
        P(("dp", "zero")),
        P(("dp", "zero")),
        P(("dp", "zero"), None),
    )
    out_specs = (P(("dp", "zero"), None), P(("dp", "zero"), None), P(None, "zero"), P())
    return jax.shard_map(shards, mesh=mesh, in_specs=in_specs, out_specs=out_specs, check_vma=False)
```

profile of v0, /device:TPU:1, one launch (start us, length us, event | category | flops | bytes accessed | tf_op | source)
XLA Modules:
  0.0 763.6 jit_solution(15845563801061688795)
XLA Ops:
  13.4 120.4 %psum.21 = f32[8]{0:T(128)S(1)} all-reduce(f32[8]{0:T(128)S(1)} %compare_select_fusion.1), channel_id=1, replica_groups=mesh['dp'=8,'zero'=96] {'dp','zero'}, use_global_device_ids=true, to_apply=%region_0.0 | all-reduce | flops 8 | bytes 64 | tf_op jit(solution)/shard_map/psum | solution.py:34
  135.4 111.1 %all-gather = bf16[96,64,7]{1,2,0:T(8,128)(2,1)S(1)} all-gather(bf16[1,64,7]{1,2,0:T(8,128)(2,1)} %bitcast.132), channel_id=1, replica_groups=mesh['dp'=8,'zero'=96] {'zero'}, dimensions={0}, use_global_device_ids=true | all-gather | bytes 86912 | tf_op jit(solution)/shard_map/all_gather | solution.py:36
  246.8 2.0 copy.41
  248.9 0.9 copy.33
  249.9 8.6 %fusion.15 = f32[128,6144]{0,1:T(8,128)S(1)} fusion(bf16[128,6144]{0,1:T(8,128)(2,1)S(1)} %copy.33, f32[128]{0:T(128)S(1)} %get-tuple-element.50, f32[6144]{0:T(1024)S(1)} %bitcast.109, f32[128]{0:T(128)S(1)} %get-tuple-element.49, f32[6144]{0:T(1024)S(1)} %bitcast.111, f32[128]{0:T(128)S(1)} %get-tuple-element.48, f32[6144]{0:T(1024)S(1)} %bitcast.113, ...), kind=kLoop, calls=%fused_computation.30 | loop fusion | flops 20447232 | bytes 14072832 | tf_op jit(solution)/shard_map/add | solution.py:44
  258.5 1.7 copy-done.1
  260.4 4.3 convolution_convert_fusion
  264.7 6.6 copy.40
  272.6 4.6 fusion.38
  277.2 2.3 multiply_convert_fusion
  279.6 1.2 fusion.39
  281.1 8.5 %fusion.24 = (f32[6144]{0:T(1024)S(1)}, f32[128,6144]{0,1:T(8,128)}, f32[6144]{0:T(1024)S(1)}, f32[128,6144]{0,1:T(8,128)}, f32[6144]{0:T(1024)S(1)}, /*index=5*/f32[128,6144]{0,1:T(8,128)}) fusion(bf16[124,6144]{0,1:T(8,128)(2,1)S(1)} %bitcast.95, f32[128]{0:T(128)S(1)} %get-tuple-element.48, f32[128,2048]{0,1:T(8,128)S(1)} %get-tuple-element.25, ...), kind=kLoop, calls=%fused_computation.39 | loop fusion | flops 10991616 | bytes 17192448 | tf_op jit(solution)/shard_map/reduce_sum | solution.py:100
  289.5 9.5 %fusion.18 = (f32[6144]{0:T(1024)S(1)}, f32[128,6144]{0,1:T(8,128)}, f32[6144]{0:T(1024)S(1)}, f32[6144]{0:T(1024)S(1)}, f32[128,6144]{0,1:T(8,128)}, /*index=5*/f32[6144]{0:T(1024)S(1)}, f32[128,6144]{0,1:T(8,128)}) fusion(bf16[127,6144]{0,1:T(8,128)(2,1)S(1)} %bitcast.98, f32[128]{0:T(128)S(1)} %get-tuple-element.45, ...), kind=kLoop, calls=%fused_computation.33 | loop fusion | flops 13344768 | bytes 18900480 | tf_op jit(solution)/shard_map/reduce_sum | solution.py:100
  299.3 2.2 copy.46
  301.7 1.3 fusion.40
  303.0 10.6 %fusion.29 = f32[128,128]{1,0:T(8,128)} fusion(f32[128,128,128]{2,1,0:T(8,128)S(1)} %fusion.40, s32[128,128]{1,0:T(8,128)S(1)} %iota_subtract_fusion, pred[128,128]{1,0:T(8,128)(4,1)S(1)} %broadcast_compare_fusion), kind=kOutput, calls=%fused_computation.52 | convolution fusion | flops 3225419776 | bytes 8536064 | tf_op jit(solution)/shard_map/dot_general | solution.py:86
  313.7 3.1 slice.165
  316.8 0.9 slice.166
  317.7 1.0 copy-done.7
  318.7 0.9 slice.167
  319.6 1.0 copy-done.11
  320.6 0.9 slice.162
  321.5 1.0 copy-done.10
  322.5 0.9 slice.163
  323.4 1.0 copy-done.9
  326.0 9.5 %add_convert_fusion = bf16[128,6144]{0,1:T(8,128)(2,1)S(1)} fusion(f32[122,6144]{0,1:T(8,128)S(1)} %slice.167, f32[123,6144]{0,1:T(8,128)S(1)} %slice.166, f32[124,6144]{0,1:T(8,128)S(1)} %slice.165, f32[125,6144]{0,1:T(8,128)S(1)} %slice.164, f32[126,6144]{0,1:T(8,128)S(1)} %slice.163, f32[127,6144]{0,1:T(8,128)S(1)} %slice.162, f32[6144]{0:T(1024)S(1)} %bitcast.110, ...), kind=kLoop, calls=%fused_computation.45 | loop fusion | flops 12582912 | bytes 23248896 | tf_op jit(solution)/shard_map/convert_element_type | solution.py:105
  335.5 1.0 copy.44
  336.5 1.6 copy.45
  338.1 375.7 %reduce-scatter.4.cloned.1.call-done = f32[64,7]{1,0:T(8,128)} async-done(((f32[6144,7]{1,0:T(8,128)}), f32[64,7]{1,0:T(8,128)}) %reduce-scatter.4.cloned.1.call-update) | async-done | bytes 1808
  714.5 26.0 %psum.22 = f32[7,64]{1,0:T(8,128)} all-reduce(f32[7,64]{1,0:T(8,128)S(1)} %copy.47), channel_id=1, replica_groups=mesh['dp'=8,'zero'=96] {'dp'}, use_global_device_ids=true, to_apply=%region_10.0 | all-reduce | flops 448 | bytes 3584 | tf_op jit(solution)/shard_map/psum | solution.py:104
  740.6 14.1 %all-reduce.19.cloned.1.call-done = f32[128,128]{1,0:T(8,128)} async-done(((f32[128,128]{1,0:T(8,128)}), f32[128,128]{1,0:T(8,128)}) %all-reduce.19.cloned.1.call-update) | async-done | bytes 65552 | tf_op jit(solution)/shard_map/psum | solution.py:102
  754.7 1.5 copy.55
  (58 shorter events, 9.8 us)
Async XLA Ops:
  8.0 241.8 %copy-start.16 = (s32[1,128]{1,0:T(1,128)S(1)}, s32[1,128]{1,0:T(1,128)}, u32[]{:S(2)}) copy-start(s32[1,128]{1,0:T(1,128)} %param.10) | copy-start | bytes 1540
  8.0 240.9 %copy-start.15 = (bf16[128,6144]{1,0:T(8,128)(2,1)S(1)}, bf16[128,6144]{1,0:T(8,128)(2,1)}, u32[]{:S(2)}) copy-start(bf16[128,6144]{1,0:T(8,128)(2,1)} %param.7) | copy-start | bytes 4718596
  8.0 705.7 %reduce-scatter.4.cloned.1.call-start = ((), (), s32[]{:S(2)}) async-start(), calls=%async_computation.2 | async-start | bytes 3178496
  249.9 10.5 %copy-start.17 = (f32[128,128]{1,0:T(8,128)S(1)}, f32[128,128]{1,0:T(8,128)}, u32[]{:S(2)}) copy-start(f32[128,128]{1,0:T(8,128)} %param.9) | copy-start | bytes 196612
  258.5 1.8 copy-start.1
  272.6 4.6 copy-start.2
  277.2 2.4 copy-start
  279.6 1.5 copy-start.12
  281.1 8.5 %copy-start.3 = (f32[128,2048]{0,1:T(8,128)}, f32[128,2048]{0,1:T(8,128)S(1)}, u32[]{:S(2)}) copy-start(f32[128,2048]{0,1:T(8,128)S(1)} %get-tuple-element.24) | copy-start | bytes 3145732
  281.1 8.5 %copy-start.5 = (f32[128,2048]{0,1:T(8,128)}, f32[128,2048]{0,1:T(8,128)S(1)}, u32[]{:S(2)}) copy-start(f32[128,2048]{0,1:T(8,128)S(1)} %get-tuple-element.25) | copy-start | bytes 3145732
  299.3 2.4 copy-start.13
  301.6 453.2 %all-reduce.19.cloned.1.call-start = ((), (), s32[]{:S(2)}) async-start(), calls=%async_computation.1 | async-start | bytes 131072 | tf_op jit(solution)/shard_map/psum | solution.py:102
  313.7 3.1 copy-start.8
  316.8 1.9 copy-start.7
  318.7 1.9 copy-start.11
  320.6 1.9 copy-start.10
  322.5 1.9 copy-start.9
  324.4 1.2 copy-start.4
  324.4 1.5 copy-start.6
  326.0 9.5 %copy-start.14 = (bf16[128,2048]{0,1:T(8,128)(2,1)S(1)}, bf16[128,2048]{0,1:T(8,128)(2,1)}, u32[]{:S(2)}) copy-start(bf16[128,2048]{0,1:T(8,128)(2,1)} %get-tuple-element.27) | copy-start | bytes 1572868
Sparse Core Ops, SparseCore 0:
  301.7 411.9 reduce-scatter.3
Sparse Core Ops, SparseCore 1:
  313.8 440.9 all-reduce.18
where the time goes:
time: 766 us; the launch traced here: 764 us
  waiting for transfers between devices  390 us (51%)
  blocking collectives  258 us (34%)
  other arithmetic  40.3 us (5%)
  local copies, waits for them, and re-layouts  36.1 us (5%)
  matrix products  22.1 us (3%)
  between operations  17.7 us (2%)
    unnamed x3, waiting for transfers between devices  376 us
    psum x1, blocking collectives, shards(): totals = lax.psum(member * counts[0].astype(jnp.float32), ('dp', 'zero'))  120 us
    all_gather x1, blocking collectives, shards(): gathered = lax.all_gather(short_filter, 'zero', axis=1, tiled=True)  111 us
    psum x1, blocking collectives, shards(): short_grad = lax.psum(zero_share, 'dp')  26 us
    reduce_sum x2, other arithmetic, shards(): jnp.sum(masked * shift_down(feats, offset).astype(jnp.float32), 0)  18 us
    unnamed x44, local copies, waits for them, and re-layouts  16.8 us
  transfers between devices with their start and end apart: 2, of which 2 were waited for; matrix products, arithmetic and copies ran while one was open for 4% of the time, Pallas kernels for 0%

commit v1 on v0

v1 whole, which is shorter than its diff:
```python
import jax
import jax.numpy as jnp
from jax import lax
from jax.experimental import pallas as pl
from jax.experimental.pallas import tpu as pltpu
from jax.sharding import Mesh, PartitionSpec as P

SHORT = 7
TILE = 128
LANES = 128
WIDTH = 256
GSIZE = 16
SUB = 8
F32, BF16 = jnp.float32, jnp.bfloat16

PARTS = (("y_hi", 2), ("x", 4), ("z", 12), ("y_lo", 4), ("core", 2))
Y = ("y_hi", "y_lo", "core")
XZ = ("x", "z")
ALL = tuple(name for name, _ in PARTS)
ZERO = ("z", "y_lo", "core")
N_Y = 16
N_Z = 12
N_YL = 4


def iota(shape, dim):
    return lax.broadcasted_iota(jnp.int32, shape, dim)


def exchange(values, axes):
    return lax.all_to_all(values, axes, 0, 0, tiled=True)


def pair_kernel(x_ref, got_ref, out_ref):
    lane = iota((SUB, LANES), 1)
    row = iota((SUB, LANES), 0)
    tiles = [got_ref[i].astype(F32) for i in range(N_Y)]
    live = tiles[0]
    for tile in tiles[1:]:
        live = live + tile
    high = jnp.floor(live * (1.0 / 64.0))
    low = pltpu.roll(live - 64.0 * high, SUB, 1)
    live = jnp.where(lane < SUB, high, jnp.where(lane < 2 * SUB, low, 0.0))
    out = jnp.zeros((SUB, LANES), F32)
    for yl in range(N_YL):
        both = jnp.where(lane < 64, tiles[2 * yl], pltpu.roll(tiles[2 * yl + 1], 64, 1))
        out = jnp.where(x_ref[0] == yl, both, out)
    out = jnp.where(row == SHORT, live, out).astype(BF16)
    for i in range(out_ref.shape[0]):
        out_ref[i] = out


def merge_kernel(got_ref, out_ref):
    total = got_ref[0].astype(F32)
    for i in range(1, N_Y):
        total = total + got_ref[i].astype(F32)
    medium = total[4 * N_Z :]
    for z in range(N_Z):
        tile = jnp.concatenate([total[4 * z : 4 * z + 4], medium, jnp.zeros((4, LANES), F32)], 0).astype(BF16)
        for x in range(out_ref.shape[0] // N_Z):
            out_ref[x * N_Z + z] = tile


def final_kernel(got_ref, short_ref, out_ref):
    total = got_ref[0].astype(F32)
    for i in range(1, got_ref.shape[0]):
        total = total + got_ref[i].astype(F32)
    short_ref[0:4, :] = total[0:4, :64]
    short_ref[4:SHORT, :] = total[0 : SHORT - 4, 64:]
    medium = total[4:12].astype(BF16)
    for i in range(out_ref.shape[0]):
        out_ref[i] = medium


def tile_kernel(
    count_ref, plan_ref, seg_ref, fq_ref, fk_ref, fv_ref, sq_ref, sk_ref, sv_ref,
    every_ref, medium_ref, cot_ref,
    mixed_ref, dfeats_ref, msg_ref,
    down_ref, up_ref, lower_ref, upper_ref, flip_ref, linked_ref, scale_ref,
    taps_ref, rtaps_ref, short_ref, med_ref, stage_ref, sems,
):
    rows, cols = iota((TILE, TILE), 0), iota((TILE, TILE), 1)
    step, steps = pl.program_id(0), pl.num_programs(0)
    halves = WIDTH // LANES
    per_half = LANES // GSIZE

    @pl.when(step == 0)
    def _():
        along = jnp.broadcast_to(seg_ref[...].astype(F32), (TILE, TILE))
        same = along == along.T
        lower_ref[...] = jnp.where(same & (rows >= cols), 1.0, 0.0)
        upper = jnp.where(same & (rows <= cols), 1.0, 0.0)
        upper_ref[...] = upper
        for j in range(1, SHORT):
            down_ref[pl.ds((j - 1) * TILE, TILE), :] = jnp.where(same & (rows - cols == j), 1.0, 0.0).astype(BF16)
            up_ref[:, pl.ds((j - 1) * TILE, TILE)] = jnp.where(same & (cols - rows == j), 1.0, 0.0).astype(BF16)
        flip = jnp.where(rows + cols == TILE - 1, 1.0, 0.0).astype(BF16)
        flip_ref[...] = flip
        linked_ref[...] = jnp.dot(flip, upper.astype(BF16), preferred_element_type=F32)
        taps = medium_ref[...].T.astype(BF16)
        taps_ref[...] = taps.astype(F32)
        rtaps_ref[...] = pltpu.roll(jnp.dot(taps, flip, preferred_element_type=F32), 1, 1)
        live = every_ref[0].astype(F32)
        for i in range(1, every_ref.shape[0]):
            live = live + every_ref[i].astype(F32)
        row8, lane8 = iota((SUB, LANES), 0), iota((SUB, LANES), 1)
        high = jnp.where((row8 == SHORT) & (lane8 == plan_ref[0]), 64.0 * live, 0.0)
        low = jnp.where((row8 == SHORT) & (lane8 == plan_ref[0] + SUB), live, 0.0)
        total = jnp.sum(jnp.sum(high + low, 0, keepdims=True), 1, keepdims=True)
        tiles = every_ref.shape[0] * N_Y
        weighting = (TILE * tiles / SUB) / jnp.broadcast_to(total, (TILE, TILE))
        scale_ref[...] = jnp.where(rows < count_ref[0], weighting, 0.0)

    slot = lax.rem(step, 2)

    def store(part, at):
        where = pl.multiple_of((part * steps + at) * WIDTH, WIDTH)
        return pltpu.make_async_copy(
            stage_ref.at[lax.rem(at, 2), part], dfeats_ref.at[:, pl.ds(where, WIDTH)],
            sems.at[lax.rem(at, 2), part],
        )

    lower = lower_ref[...] > 0.5
    upper = upper_ref[...] > 0.5
    linked = linked_ref[...] > 0.5
    scale = jnp.concatenate([scale_ref[...]] * halves, 1)
    living = iota((TILE, WIDTH), 0) < count_ref[0]
    lane_group = iota((TILE, LANES), 1) // GSIZE

    def conv(f_ref, s_ref):
        feats = f_ref[...]
        taps = jnp.concatenate([s_ref[h, 0].astype(F32) for h in range(halves)], 1)
        shifted = jnp.dot(down_ref[...], feats, preferred_element_type=F32)
        total = feats.astype(F32) * taps[0:1]
        for j in range(1, SHORT):
            total = total + shifted[(j - 1) * TILE : j * TILE] * taps[j : j + 1]
        return total, shifted, taps

    query, q_shift, q_taps = conv(fq_ref, sq_ref)
    key, k_shift, k_taps = conv(fk_ref, sk_ref)
    value, v_shift, v_taps = conv(fv_ref, sv_ref)
    product = (key * value).astype(BF16)
    flipped = jnp.dot(flip_ref[...], product, preferred_element_type=F32).astype(BF16)
    gout = cot_ref[...].astype(F32) * scale
    glong = (gout * query).astype(BF16)
    zero = jnp.zeros((TILE, LANES), BF16)
    taps_here = taps_ref[pl.ds(pl.multiple_of(step * halves * per_half, halves * per_half), halves * per_half), :]
    rtaps_here = rtaps_ref[pl.ds(pl.multiple_of(step * halves * per_half, halves * per_half), halves * per_half), :]

    longs, gprods = [], []
    for half in range(halves):
        lanes = slice(half * LANES, (half + 1) * LANES)
        prod_half, glong_half, flip_half = product[:, lanes], glong[:, lanes], flipped[:, lanes]
        forward, backward, prods, glongs, flips = [], [], [], [], []
        for g in range(per_half):
            row = half * per_half + g
            base = jnp.broadcast_to(rtaps_here[row : row + 1, :], (TILE, TILE))
            forward.append(
                jnp.where(lower, pltpu.roll(base, 0, 1, stride=1, stride_axis=0), 0.0).astype(BF16)
            )
            base = jnp.broadcast_to(taps_here[row : row + 1, :], (TILE, TILE))
            backward.append(
                jnp.where(upper, pltpu.roll(base, 0, 1, stride=1, stride_axis=0), 0.0).astype(BF16)
            )
            prods.append(jnp.where(lane_group == g, prod_half, zero))
            glongs.append(jnp.where(lane_group == g, glong_half, zero))
            flips.append(jnp.where(lane_group == g, flip_half, zero))
        longs.append(
            jnp.dot(jnp.concatenate(forward, 1), jnp.concatenate(prods, 0), preferred_element_type=F32)
        )
        gprods.append(
            jnp.dot(jnp.concatenate(backward, 1), jnp.concatenate(glongs, 0), preferred_element_type=F32)
        )
        crossed = lax.dot_general(
            jnp.concatenate(flips, 0), glong_half, (((1,), (1,)), ((), ())), preferred_element_type=F32
        )
        sums = []
        for g in range(per_half):
            part = jnp.where(linked, crossed[g * TILE : (g + 1) * TILE], 0.0)
            part = pltpu.roll(part, 1, 1, stride=1, stride_axis=0)
            sums.append(jnp.sum(part, 0, keepdims=True))
        med_ref[halves * step + half] = jnp.concatenate(sums, 0)
    long_conv = jnp.concatenate(longs, 1)
    gprod = jnp.concatenate(gprods, 1)
    mixed_ref[...] = jnp.where(living, query * long_conv, 0.0).astype(BF16)

    @pl.when(step >= 2)
    def _():
        for part in range(3):
            store(part, step - 2).wait()

    row8, lane8 = iota((SUB, LANES), 0), iota((SUB, LANES), 1)
    keep = (row8 < 4) == (lane8 < 64)

    def unconv(part, grad, f_ref, taps, shifted):
        sums = [jnp.sum(grad * f_ref[...].astype(F32), 0, keepdims=True)]
        parts = []
        for j in range(1, SHORT):
            sums.append(jnp.sum(grad * shifted[(j - 1) * TILE : j * TILE], 0, keepdims=True))
            parts.append((grad * taps[j : j + 1]).astype(BF16))
        sums.append(jnp.zeros((1, WIDTH), F32))
        sums = jnp.concatenate(sums, 0)
        z = part * (N_Z // 3) + step // 2
        for h in range(halves):
            tile = sums[:, h * LANES : (h + 1) * LANES]
            other = pltpu.roll(pltpu.roll(tile, 64, 1), 4, 0)
            short_ref[z * N_YL + lax.rem(step, 2) * halves + h] = jnp.where(keep, tile, other)
        back = jnp.dot(up_ref[...], jnp.concatenate(parts, 0), preferred_element_type=F32)
        stage_ref[slot, part] = (grad * taps[0:1] + back).astype(BF16)
        store(part, step).start()

    unconv(0, gout * long_conv, fq_ref, q_taps, q_shift)
    unconv(1, gprod * value, fk_ref, k_taps, k_shift)
    unconv(2, gprod * key, fv_ref, v_taps, v_shift)

    @pl.when(step == steps - 1)
    def _():
        medium = jnp.concatenate([med_ref[i] for i in range(2 * halves * 4)], 0).T
        for yl in range(N_YL):
            for core in range(2):
                tiles = [short_ref[z * N_YL + yl][4 * core : 4 * core + 4] for z in range(N_Z)]
                for yh in range(2):
                    to = yh * 2 * N_YL + yl * 2 + core
                    msg_ref[to] = jnp.concatenate(tiles + [medium[to * SUB : (to + 1) * SUB]], 0).astype(BF16)
        for at in (steps - 2, steps - 1):
            for part in range(3):
                store(part, at).wait()


def whole(shape):
    return pl.BlockSpec(shape, lambda *_: (0,) * len(shape))


def tile_call(count, plan, doc_ids, feats, filters, medium, cotangent):
    width = cotangent.shape[1]
    steps = width // WIDTH
    halves = WIDTH // LANES
    groups = medium.shape[1]
    smem = pl.BlockSpec(memory_space=pltpu.SMEM)

    def block(part=0):
        return pl.BlockSpec((TILE, WIDTH), lambda i, part=part: (0, part * steps + i))

    def taps(part):
        return pl.BlockSpec(
            (halves, 1, SUB, LANES), lambda i, part=part: (lax.rem(i, 2), part * (N_Z // 3) + i // 2, 0, 0)
        )

    every = filters.reshape(N_YL * N_Z, SUB, LANES)
    vmem = pltpu.VMEM
    return pl.pallas_call(
        tile_kernel,
        grid=(steps,),
        in_specs=[
            smem, smem, whole((1, TILE)), block(0), block(1), block(2), taps(0), taps(1), taps(2),
            whole(every.shape), whole(medium.shape), block(0),
        ],
        out_specs=[
            block(0), pl.BlockSpec(memory_space=pl.ANY), whole((N_Y, 4 * N_Z + SUB, LANES)),
        ],
        out_shape=[
            jax.ShapeDtypeStruct(cotangent.shape, BF16),
            jax.ShapeDtypeStruct(feats.shape, BF16),
            jax.ShapeDtypeStruct((N_Y, 4 * N_Z + SUB, LANES), BF16),
        ],
        scratch_shapes=[
            vmem(((SHORT - 1) * TILE, TILE), BF16),
            vmem((TILE, (SHORT - 1) * TILE), BF16),
            vmem((TILE, TILE), F32),
            vmem((TILE, TILE), F32),
            vmem((TILE, TILE), BF16),
            vmem((TILE, TILE), F32),
            vmem((TILE, TILE), F32),
            vmem((groups, TILE), F32),
            vmem((groups, TILE), F32),
            vmem((N_Z * N_YL, SUB, LANES), F32),
            vmem((groups // SUB, SUB, TILE), F32),
            vmem((2, 3, TILE, WIDTH), BF16),
            pltpu.SemaphoreType.DMA((2, 3)),
        ],
        name="tile",
    )(count, plan, doc_ids, feats, feats, feats, filters, filters, filters, every, medium, cotangent)


def small_call(kernel, outs, *operands, name):
    in_specs = [
        pl.BlockSpec(memory_space=pltpu.SMEM if x.dtype == jnp.int32 else pltpu.VMEM) for x in operands
    ]
    return pl.pallas_call(
        kernel,
        in_specs=in_specs,
        out_specs=[pl.BlockSpec(memory_space=pltpu.VMEM)] * len(outs),
        out_shape=[jax.ShapeDtypeStruct(*o) for o in outs],
        name=name,
    )(*operands)


def gather_filters(short_filter, counts, plan):
    n_xz = lax.axis_size("x") * N_Z
    lane = iota((SUB, LANES), 1)
    row = iota((SUB, LANES), 0)
    padded = jnp.pad(short_filter, ((0, SUB - SHORT), (0, LANES - short_filter.shape[1])))
    member = jnp.where(lane == plan[0], counts[0], 0).astype(BF16)
    tile = jnp.where(row == SHORT, member, padded)
    got = exchange(jnp.broadcast_to(tile[None], (N_Y, SUB, LANES)), Y)
    where = lax.axis_index("x").astype(jnp.int32).reshape(1)
    (send,) = small_call(pair_kernel, [((n_xz, SUB, LANES), BF16)], where, got, name="pair")
    return exchange(send, XZ).reshape(N_YL, N_Z, SUB, LANES)


def reduce_grads(message):
    n_xz = lax.axis_size("x") * N_Z
    got = exchange(message, Y)
    (send,) = small_call(merge_kernel, [((n_xz, 16, LANES), BF16)], got, name="merge")
    got = exchange(send, XZ)
    short_grad, send = small_call(
        final_kernel, [((SHORT, 64), F32), ((N_Y, SUB, LANES), BF16)], got, name="final"
    )
    return short_grad, exchange(send, Y).reshape(TILE, LANES).astype(F32)


def shards(feats, short_filter, medium_filter, doc_ids, counts, plan, cotangent):
    filters = gather_filters(short_filter, counts, plan)
    mixed, feats_grad, message = tile_call(counts, plan, doc_ids, feats, filters, medium_filter, cotangent)
    short_grad, medium_grad = reduce_grads(message)
    return mixed, feats_grad, short_grad, medium_grad


def solution(mesh):
    parts = Mesh(mesh.devices.reshape([size for _, size in PARTS]), ALL)
    in_specs = (P(ALL, None), P(None, ZERO), P(), P(ALL, None), P(ALL), P(ALL), P(ALL, None))
    out_specs = (P(ALL, None), P(ALL, None), P(None, ZERO), P())
    return jax.shard_map(shards, mesh=parts, in_specs=in_specs, out_specs=out_specs, check_vma=False)
```

time: 766 us -> 124 us (0.16)
  waiting for transfers between devices: 390 us -> 7.48 us
  blocking collectives: 258 us -> 74.1 us
  other arithmetic: 40.3 us -> 1.4 us
  local copies, waits for them, and re-layouts: 36.1 us -> 1.24 us
  Pallas kernels: 0 us -> 23.6 us
  matrix products: 22.1 us -> 0 us
  between operations: 17.7 us -> 1.95 us
  starting transfers between devices: 0.08 us -> 13.8 us
    unnamed x3 -> x0, waiting for transfers between devices: 376 us -> none
    psum x2 -> x0, blocking collectives: 146 us -> none  [the longest x1 120 us: shards(): totals = lax.psum(member * counts[0].astype(jnp.float32), ('dp', 'zero'))]
    all_gather x1 -> x0, blocking collectives: 111 us -> none  [shards(): gathered = lax.all_gather(short_filter, 'zero', axis=1, tiled=True)]
    all_to_all x0 -> x4, blocking collectives: none -> 74.1 us  [exchange(): return lax.all_to_all(values, axes, 0, 0, tiled=True)]
    pallas_call x0 -> x4, Pallas kernels: none -> 23.6 us  [the longest x1 18.8 us: tile_call(): pl.pallas_call(tile_kernel, grid=(steps,), in_specs=[smem, smem, whole((1...]
    dot_general x5 -> x0, matrix products: 22.1 us -> none  [the longest x1 10.6 us: shards(): lax.dot_general(crossed, selector.astype(jnp.float32), (((1,), (1,)), (()...]
    reduce_sum x3 -> x0, other arithmetic: 18.6 us -> none  [the longest x2 18 us: shards(): jnp.sum(masked * shift_down(feats, offset).astype(jnp.float32), 0)]
    unnamed x44 -> x2, local copies, waits for them, and re-layouts: 16.8 us -> 0.61 us
  transfers between devices with their start and end apart: 2 -> 1, of which waited for: 2 -> 1; matrix products, arithmetic and copies ran while one was open for 4% -> 0% of each run, Pallas kernels for 0% -> 0%
where the time goes in v1:
time: 124 us; the launch traced here: 123 us
  blocking collectives  74.1 us (60%)
  Pallas kernels  23.6 us (19%)
  starting transfers between devices  13.8 us (11%)
  waiting for transfers between devices  7.48 us (6%)
  between operations  1.95 us (2%)
  other arithmetic  1.4 us (1%)
  local copies, waits for them, and re-layouts  1.24 us (1%)
    all_to_all x4, blocking collectives, exchange(): return lax.all_to_all(values, axes, 0, 0, tiled=True)  74.1 us
    pallas_call x1, Pallas kernels, tile_call(): pl.pallas_call(tile_kernel, grid=(steps,), in_specs=[smem, smem, whole((1...  18.8 us
    all_to_all x1, starting transfers between devices, exchange(): return lax.all_to_all(values, axes, 0, 0, tiled=True)  13.8 us
    all_to_all x1, waiting for transfers between devices, exchange(): return lax.all_to_all(values, axes, 0, 0, tiled=True)  7.48 us
    pallas_call x3, Pallas kernels, small_call(): pl.pallas_call(kernel, in_specs=in_specs, out_specs=[pl.BlockSpec(memory_...  4.79 us
  transfers between devices with their start and end apart: 1, of which 1 were waited for; matrix products, arithmetic and copies ran while one was open for 0% of the time, Pallas kernels for 0%

profile of v1, /device:TPU:1, one launch (start us, length us, event | category | flops | bytes accessed | tf_op | source)
XLA Modules:
  0.0 123.5 jit_solution(16813999156275239149)
XLA Ops:
  1.9 0.8 pad_select_fusion
  2.7 0.6 broadcast_in_dim.16
  3.3 13.8 %all-to-all-start = ((bf16[16,8,128]{2,1,0:T(8,128)(2,1)}), bf16[16,8,128]{2,1,0:T(8,128)(2,1)S(1)}, u32[]{:S(2)}, u32[]{:S(2)}) async-start(bf16[16,8,128]{2,1,0:T(8,128)(2,1)} %broadcast_in_dim.16), calls=%async_computation | async-start | bytes 65536 | tf_op jit(solution)/shard_map/all_to_all | solution.py:31
  17.1 7.5 %all-to-all-done.got_ref = bf16[16,8,128]{2,1,0:T(8,128)(2,1)S(1)} async-done(((bf16[16,8,128]{2,1,0:T(8,128)(2,1)}), bf16[16,8,128]{2,1,0:T(8,128)(2,1)S(1)}, u32[]{:S(2)}, u32[]{:S(2)}) %all-to-all-start) | async-done | bytes 32800 | tf_op jit(solution)/shard_map/all_to_all | solution.py:31
  24.6 0.0 copy-start
  24.6 0.6 copy-done
  25.2 1.5 %pair.1 = bf16[48,8,128]{2,1,0:T(8,128)(2,1)} custom-call(s32[1]{0:T(128)} %bitcast.x_ref, bf16[16,8,128]{2,1,0:T(8,128)(2,1)} %copy-done), custom_call_target="tpu_custom_call" | custom-call | tf_op jit(solution)/shard_map/pair/pallas_call | solution.py:289
  26.7 24.8 %all_to_all.25.every_ref = bf16[48,8,128]{2,1,0:T(8,128)(2,1)} all-to-all(bf16[48,8,128]{2,1,0:T(8,128)(2,1)} %pair.1), channel_id=1, replica_groups=mesh['y_hi'=2,'x'=4,'z'=12,'y_lo'=4,'core'=2] {'x','z'}, dimensions={0} | all-to-all | bytes 196608 | tf_op jit(solution)/shard_map/all_to_all | solution.py:31
  51.5 18.8 %tile.1 = (bf16[128,2048]{1,0:T(8,128)(2,1)}, bf16[128,6144]{1,0:T(8,128)(2,1)}, bf16[16,56,128]{2,1,0:T(8,128)(2,1)}) custom-call(s32[1]{0:T(128)} %copy.11.count_ref, s32[1]{0:T(128)} %copy.12.plan_ref, s32[1,128]{1,0:T(1,128)} %seg_ref.1, bf16[128,6144]{1,0:T(8,128)(2,1)} %fv_ref.1, bf16[128,6144]{1,0:T(8,128)(2,1)} %fv_ref.1, bf16[128,6144]{1,0:T(8,128)(2,1)} %fv_ref.1, ...), custom_call_target="tpu_custom_call" | custom-call | tf_op jit(solution)/shard_map/tile/pallas_call | solution.py:251
  70.2 17.4 %all_to_all.26.got_ref = bf16[16,56,128]{2,1,0:T(8,128)(2,1)} all-to-all(bf16[16,56,128]{2,1,0:T(8,128)(2,1)} %get-tuple-element.11), channel_id=1, replica_groups=mesh['y_hi'=2,'x'=4,'z'=12,'y_lo'=4,'core'=2] {'y_hi','y_lo','core'}, dimensions={0} | all-to-all | bytes 458752 | tf_op jit(solution)/shard_map/all_to_all | solution.py:31
  87.6 1.7 %merge.1 = bf16[48,16,128]{2,1,0:T(8,128)(2,1)} custom-call(bf16[16,56,128]{2,1,0:T(8,128)(2,1)} %all_to_all.26.got_ref), custom_call_target="tpu_custom_call" | custom-call | tf_op jit(solution)/shard_map/merge/pallas_call | solution.py:289
  89.3 20.8 %all_to_all.27.got_ref = bf16[48,16,128]{2,1,0:T(8,128)(2,1)} all-to-all(bf16[48,16,128]{2,1,0:T(8,128)(2,1)} %merge.1), channel_id=1, replica_groups=mesh['y_hi'=2,'x'=4,'z'=12,'y_lo'=4,'core'=2] {'x','z'}, dimensions={0} | all-to-all | bytes 393216 | tf_op jit(solution)/shard_map/all_to_all | solution.py:31
  110.1 1.6 %final.1 = (f32[7,64]{1,0:T(8,128)}, bf16[16,8,128]{2,1,0:T(8,128)(2,1)}) custom-call(bf16[48,16,128]{2,1,0:T(8,128)(2,1)} %all_to_all.27.got_ref), custom_call_target="tpu_custom_call" | custom-call | tf_op jit(solution)/shard_map/final/pallas_call | solution.py:289
  111.7 11.2 %all_to_all.28 = bf16[16,8,128]{2,1,0:T(8,128)(2,1)S(1)} all-to-all(bf16[16,8,128]{2,1,0:T(8,128)(2,1)} %get-tuple-element.13), channel_id=1, replica_groups=mesh['y_hi'=2,'x'=4,'z'=12,'y_lo'=4,'core'=2] {'y_hi','y_lo','core'}, dimensions={0} | all-to-all | bytes 65536 | tf_op jit(solution)/shard_map/all_to_all | solution.py:31
  122.9 0.6 bitcast_convert_fusion
  (2 shorter events, 0.0 us)
Async XLA Ops:
  3.3 21.2 %all-to-all-start = ((bf16[16,8,128]{2,1,0:T(8,128)(2,1)}), bf16[16,8,128]{2,1,0:T(8,128)(2,1)S(1)}, u32[]{:S(2)}, u32[]{:S(2)}) async-start(bf16[16,8,128]{2,1,0:T(8,128)(2,1)} %broadcast_in_dim.16), calls=%async_computation | async-start | bytes 65536 | tf_op jit(solution)/shard_map/all_to_all | solution.py:31
  24.6 0.6 copy-start

commit v2 on v1

v2 whole, which is shorter than its diff:
```python
import jax
import jax.numpy as jnp
from jax import lax
from jax.experimental import pallas as pl
from jax.experimental.pallas import tpu as pltpu
from jax.sharding import Mesh, PartitionSpec as P

SHORT = 7
TILE = 128
LANES = 128
WIDTH = 512
PER_Z = 512 // WIDTH
GSIZE = 16
SUB = 8
RANKS = 8
F32, BF16 = jnp.float32, jnp.bfloat16

PARTS = (("y_hi", 2), ("x_hi", 2), ("x_lo", 2), ("z", 12), ("y_lo", 4), ("core", 2))
Y = ("y_hi", "y_lo", "core")
X = ("x_hi", "x_lo")
XZ = X + ("z",)
SHARE = ("x_lo",) + Y
ALL = tuple(name for name, _ in PARTS)
ZERO = ("z", "y_lo", "core")
N_Y = 16
N_Z = 12
N_YL = 4
N_X = 4


def iota(shape, dim):
    return lax.broadcasted_iota(jnp.int32, shape, dim)


def exchange(values, axes):
    return lax.all_to_all(values, axes, 0, 0, tiled=True)


def pair_kernel(x_ref, got_ref, out_ref):
    lane = iota((SUB, LANES), 1)
    row = iota((SUB, LANES), 0)
    tiles = [got_ref[i].astype(F32) for i in range(N_Y)]
    live = tiles[0]
    for tile in tiles[1:]:
        live = live + tile
    high = jnp.floor(live * (1.0 / 64.0))
    low = pltpu.roll(live - 64.0 * high, SUB, 1)
    live = jnp.where(lane < SUB, high, jnp.where(lane < 2 * SUB, low, 0.0))
    out = jnp.zeros((SUB, LANES), F32)
    for yl in range(N_YL):
        both = jnp.where(lane < 64, tiles[2 * yl], pltpu.roll(tiles[2 * yl + 1], 64, 1))
        out = jnp.where(x_ref[0] == yl, both, out)
    out = jnp.where(row == SHORT, live, out).astype(BF16)
    for i in range(out_ref.shape[0]):
        out_ref[i] = out


def merge_kernel(got_ref, out_ref):
    total = got_ref[0].astype(F32)
    for i in range(1, N_Y):
        total = total + got_ref[i].astype(F32)
    for xl in range(2):
        medium = total[4 * N_Z + 4 * xl : 4 * N_Z + 4 * xl + 4]
        for z in range(N_Z):
            tile = jnp.concatenate([total[4 * z : 4 * z + 4], medium], 0).astype(BF16)
            for xh in range(N_X // 2):
                out_ref[(2 * xh + xl) * N_Z + z] = tile


def final_kernel(got_ref, short_ref, out_ref):
    total = got_ref[0].astype(F32)
    for i in range(1, got_ref.shape[0]):
        total = total + got_ref[i].astype(F32)
    short_ref[0:4, :] = total[0:4, :64]
    short_ref[4:SHORT, :] = total[0 : SHORT - 4, 64:]
    medium = total[4:]
    for i in range(out_ref.shape[0]):
        out_ref[i] = medium


def prepare_kernel(seg_ref, medium_ref, down_ref, up_ref, linked_ref, forward_ref, backward_ref, taps_ref, rtaps_ref):
    rows, cols = iota((TILE, TILE), 0), iota((TILE, TILE), 1)
    along = jnp.broadcast_to(seg_ref[...].astype(F32), (TILE, TILE))
    same = along == along.T
    lower, upper = same & (rows >= cols), same & (rows <= cols)

    @pl.when(pl.program_id(0) == 0)
    def _():
        for j in range(1, SHORT):
            down_ref[pl.ds((j - 1) * TILE, TILE), :] = jnp.where(same & (rows - cols == j), 1.0, 0.0).astype(BF16)
            up_ref[pl.ds((j - 1) * TILE, TILE), :] = jnp.where(same & (cols - rows == j), 1.0, 0.0).astype(BF16)
        flip = jnp.where(rows + cols == TILE - 1, 1.0, 0.0).astype(BF16)
        down_ref[pl.ds((SHORT - 1) * TILE, TILE), :] = flip
        linked_ref[...] = jnp.dot(flip, jnp.where(upper, 1.0, 0.0).astype(BF16), preferred_element_type=F32)
        taps = medium_ref[...].T.astype(BF16)
        taps_ref[...] = taps.astype(F32)
        rtaps_ref[...] = pltpu.roll(jnp.dot(taps, flip, preferred_element_type=F32), 1, 1)

    n = forward_ref.shape[1] // TILE
    at = pl.ds(pl.multiple_of(pl.program_id(0) * n, n), n)
    taps, rtaps = taps_ref[at, :], rtaps_ref[at, :]
    for g in range(n):
        where = slice(g * TILE, (g + 1) * TILE)
        base = jnp.broadcast_to(rtaps[g : g + 1, :], (TILE, TILE))
        base = pltpu.roll(base, 0, 1, stride=1, stride_axis=0)
        forward_ref[:, where] = jnp.where(lower, base, 0.0).astype(BF16)
        base = jnp.broadcast_to(taps[g : g + 1, :], (TILE, TILE))
        base = pltpu.roll(base, 0, 1, stride=1, stride_axis=0)
        backward_ref[:, where] = jnp.where(upper, base, 0.0).astype(BF16)


def tile_kernel(
    count_ref, plan_ref, fq_ref, fk_ref, fv_ref, sq_ref, sk_ref, sv_ref,
    every_ref, down_ref, linked_ref, forward_ref, backward_ref, cot_ref,
    mixed_ref, gq_ref, gk_ref, gv_ref, msg_ref,
    scale_ref, short_ref, med_ref,
):
    rows = iota((TILE, TILE), 0)
    step, steps = pl.program_id(0), pl.num_programs(0)
    halves = WIDTH // LANES
    per_half = LANES // GSIZE

    @pl.when(step == 0)
    def _():
        live = every_ref[0].astype(F32)
        for i in range(1, every_ref.shape[0]):
            live = live + every_ref[i].astype(F32)
        row8, lane8 = iota((SUB, LANES), 0), iota((SUB, LANES), 1)
        high = jnp.where((row8 == SHORT) & (lane8 == plan_ref[0]), 64.0 * live, 0.0)
        low = jnp.where((row8 == SHORT) & (lane8 == plan_ref[0] + RANKS), live, 0.0)
        total = jnp.sum(jnp.sum(high + low, 0, keepdims=True), 1, keepdims=True)
        tiles = every_ref.shape[0] * N_Y
        weighting = (TILE * tiles / RANKS) / jnp.broadcast_to(total, (TILE, TILE))
        scale_ref[...] = jnp.where(rows < count_ref[0], weighting, 0.0)

    linked = linked_ref[...] > 0.5
    scale = jnp.concatenate([scale_ref[...]] * halves, 1)
    living = iota((TILE, WIDTH), 0) < count_ref[0]
    lane_group = iota((TILE, LANES), 1) // GSIZE

    def conv(f_ref, s_ref):
        feats = f_ref[...]
        taps = jnp.concatenate([s_ref[h, 0].astype(F32) for h in range(halves)], 1)
        shifted = jnp.dot(down_ref[: (SHORT - 1) * TILE], feats, preferred_element_type=F32)
        total = feats.astype(F32) * taps[0:1]
        for j in range(1, SHORT):
            total = total + shifted[(j - 1) * TILE : j * TILE] * taps[j : j + 1]
        return total, shifted

    query, q_shift = conv(fq_ref, sq_ref)
    key, k_shift = conv(fk_ref, sk_ref)
    value, v_shift = conv(fv_ref, sv_ref)
    product = (key * value).astype(BF16)
    flipped = jnp.dot(down_ref[(SHORT - 1) * TILE :], product, preferred_element_type=F32).astype(BF16)
    gout = cot_ref[...].astype(F32) * scale
    glong = (gout * query).astype(BF16)
    zero = jnp.zeros((TILE, LANES), BF16)

    longs, gprods = [], []
    for half in range(halves):
        lanes = slice(half * LANES, (half + 1) * LANES)
        blocks = slice(half * per_half * TILE, (half + 1) * per_half * TILE)
        prod_half, glong_half, flip_half = product[:, lanes], glong[:, lanes], flipped[:, lanes]
        prods, glongs, flips = [], [], []
        for g in range(per_half):
            prods.append(jnp.where(lane_group == g, prod_half, zero))
            glongs.append(jnp.where(lane_group == g, glong_half, zero))
            flips.append(jnp.where(lane_group == g, flip_half, zero))
        longs.append(jnp.dot(forward_ref[:, blocks], jnp.concatenate(prods, 0), preferred_element_type=F32))
        gprods.append(jnp.dot(backward_ref[:, blocks], jnp.concatenate(glongs, 0), preferred_element_type=F32))
        crossed = lax.dot_general(
            jnp.concatenate(flips, 0), glong_half, (((1,), (1,)), ((), ())), preferred_element_type=F32
        )
        sums = []
        for g in range(per_half):
            part = jnp.where(linked, crossed[g * TILE : (g + 1) * TILE], 0.0)
            part = pltpu.roll(part, 1, 1, stride=1, stride_axis=0)
            sums.append(jnp.sum(part, 0, keepdims=True))
        med_ref[halves * step + half] = jnp.concatenate(sums, 0)
    long_conv = jnp.concatenate(longs, 1)
    gprod = jnp.concatenate(gprods, 1)
    mixed_ref[...] = jnp.where(living, query * long_conv, 0.0).astype(BF16)

    row8, lane8 = iota((SUB, LANES), 0), iota((SUB, LANES), 1)
    keep = (row8 < 4) == (lane8 < 64)

    def taps_grad(part, grad, f_ref, shifted, g_ref):
        g_ref[...] = grad.astype(BF16)
        sums = [jnp.sum(grad * f_ref[...].astype(F32), 0, keepdims=True)]
        for j in range(1, SHORT):
            sums.append(jnp.sum(grad * shifted[(j - 1) * TILE : j * TILE], 0, keepdims=True))
        sums.append(jnp.zeros((1, WIDTH), F32))
        sums = jnp.concatenate(sums, 0)
        z = part * (N_Z // 3) + step // PER_Z
        for h in range(halves):
            tile = sums[:, h * LANES : (h + 1) * LANES]
            other = pltpu.roll(pltpu.roll(tile, 64, 1), 4, 0)
            short_ref[z * N_YL + lax.rem(step, PER_Z) * halves + h] = jnp.where(keep, tile, other)

    taps_grad(0, gout * long_conv, fq_ref, q_shift, gq_ref)
    taps_grad(1, gprod * value, fk_ref, k_shift, gk_ref)
    taps_grad(2, gprod * key, fv_ref, v_shift, gv_ref)

    @pl.when(step == steps - 1)
    def _():
        medium = jnp.concatenate([med_ref[i] for i in range(med_ref.shape[0])], 0).T
        for yl in range(N_YL):
            for core in range(2):
                tiles = [short_ref[z * N_YL + yl][4 * core : 4 * core + 4] for z in range(N_Z)]
                for yh in range(2):
                    to = yh * 2 * N_YL + yl * 2 + core
                    pieces = [medium[64 * xl + 4 * to : 64 * xl + 4 * to + 4] for xl in range(2)]
                    msg_ref[to] = jnp.concatenate(tiles + pieces, 0).astype(BF16)


def spread_kernel(gq_ref, gk_ref, gv_ref, sq_ref, sk_ref, sv_ref, up_ref, dfeats_ref, stage_ref, sems):
    step, steps = pl.program_id(0), pl.num_programs(0)
    width = gq_ref.shape[1]

    def store(part, at):
        where = pl.multiple_of((part * steps + at) * width, width)
        return pltpu.make_async_copy(
            stage_ref.at[lax.rem(at, 2), part], dfeats_ref.at[:, pl.ds(where, width)], sems.at[lax.rem(at, 2), part]
        )

    @pl.when(step >= 2)
    def _():
        for part in range(3):
            store(part, step - 2).wait()

    for part, (g_ref, s_ref) in enumerate(((gq_ref, sq_ref), (gk_ref, sk_ref), (gv_ref, sv_ref))):
        grad = g_ref[...]
        taps = jnp.concatenate([s_ref[h, 0].astype(F32) for h in range(s_ref.shape[0])], 1)
        shifted = jnp.dot(up_ref[...], grad, preferred_element_type=F32)
        total = grad.astype(F32) * taps[0:1]
        for j in range(1, SHORT):
            total = total + shifted[(j - 1) * TILE : j * TILE] * taps[j : j + 1]
        stage_ref[lax.rem(step, 2), part] = total.astype(BF16)
        store(part, step).start()

    @pl.when(step == steps - 1)
    def _():
        for at in (steps - 2, steps - 1):
            for part in range(3):
                store(part, at).wait()


def whole(shape):
    return pl.BlockSpec(shape, lambda *_: (0,) * len(shape))


def block(rows=TILE, part=0, steps=0):
    return pl.BlockSpec((rows, WIDTH), lambda i: (0, part * steps + i))


def taps_block(part):
    return pl.BlockSpec((WIDTH // LANES, 1, SUB, LANES), lambda i: (lax.rem(i, PER_Z), part * (N_Z // 3) + i // PER_Z, 0, 0))


SMEM = pl.BlockSpec(memory_space=pltpu.SMEM)


def prepare_call(doc_ids, medium):
    groups = medium.shape[1]
    n = 16
    rows = pl.BlockSpec((TILE, n * TILE), lambda i: (0, i))
    return pl.pallas_call(
        prepare_kernel,
        grid=(groups // n,),
        in_specs=[whole((1, TILE)), whole(medium.shape)],
        out_specs=[whole((SHORT * TILE, TILE)), whole(((SHORT - 1) * TILE, TILE)), whole((TILE, TILE)), rows, rows],
        out_shape=[
            jax.ShapeDtypeStruct((SHORT * TILE, TILE), BF16),
            jax.ShapeDtypeStruct(((SHORT - 1) * TILE, TILE), BF16),
            jax.ShapeDtypeStruct((TILE, TILE), F32),
            jax.ShapeDtypeStruct((TILE, groups * TILE), BF16),
            jax.ShapeDtypeStruct((TILE, groups * TILE), BF16),
        ],
        scratch_shapes=[pltpu.VMEM((groups, TILE), F32), pltpu.VMEM((groups, TILE), F32)],
        name="prepare",
    )(doc_ids, medium)


def tile_call(count, plan, feats, filters, down, linked, forward, backward, cotangent):
    width = cotangent.shape[1]
    steps = width // WIDTH
    every = filters.reshape(N_YL * N_Z, SUB, LANES)
    toeplitz = pl.BlockSpec((TILE, forward.shape[1] // steps), lambda i: (0, i))
    message = (N_Y, 4 * N_Z + SUB, LANES)
    vmem = pltpu.VMEM
    part = jax.ShapeDtypeStruct(cotangent.shape, BF16)
    return pl.pallas_call(
        tile_kernel,
        grid=(steps,),
        in_specs=[SMEM, SMEM]
        + [block(TILE, p, steps) for p in range(3)]
        + [taps_block(p) for p in range(3)]
        + [whole(every.shape), whole(down.shape), whole(linked.shape), toeplitz, toeplitz, block()],
        out_specs=[block(), block(), block(), block(), whole(message)],
        out_shape=[part, part, part, part, jax.ShapeDtypeStruct(message, BF16)],
        scratch_shapes=[
            vmem((TILE, TILE), F32),
            vmem((N_Z * N_YL, SUB, LANES), F32),
            vmem((forward.shape[1] // TILE // SUB, SUB, TILE), F32),
        ],
        name="tile",
    )(count, plan, feats, feats, feats, filters, filters, filters, every, down, linked, forward, backward, cotangent)


def spread_call(grads, filters, up):
    width = grads[0].shape[1]
    steps = width // WIDTH
    return pl.pallas_call(
        spread_kernel,
        grid=(steps,),
        in_specs=[block()] * 3 + [taps_block(p) for p in range(3)] + [whole(up.shape)],
        out_specs=pl.BlockSpec(memory_space=pl.ANY),
        out_shape=jax.ShapeDtypeStruct((TILE, 3 * width), BF16),
        scratch_shapes=[pltpu.VMEM((2, 3, TILE, WIDTH), BF16), pltpu.SemaphoreType.DMA((2, 3))],
        name="spread",
    )(*grads, filters, filters, filters, up)


def small_call(kernel, outs, *operands):
    in_specs = [
        pl.BlockSpec(memory_space=pltpu.SMEM if x.dtype == jnp.int32 else pltpu.VMEM) for x in operands
    ]
    return pl.pallas_call(
        kernel,
        in_specs=in_specs,
        out_specs=[pl.BlockSpec(memory_space=pltpu.VMEM)] * len(outs),
        out_shape=[jax.ShapeDtypeStruct(*o) for o in outs],
    )(*operands)


def gather_filters(short_filter, counts, plan):
    n_xz = N_X * N_Z
    lane = iota((SUB, LANES), 1)
    row = iota((SUB, LANES), 0)
    padded = jnp.pad(short_filter, ((0, SUB - SHORT), (0, LANES - short_filter.shape[1])))
    member = jnp.where(lane == plan[0], counts[0], 0).astype(BF16)
    tile = jnp.where(row == SHORT, member, padded)
    got = exchange(jnp.broadcast_to(tile[None], (N_Y, SUB, LANES)), Y)
    where = lax.axis_index(X).astype(jnp.int32).reshape(1)
    (send,) = small_call(pair_kernel, [((n_xz, SUB, LANES), BF16)], where, got)
    return exchange(send, XZ).reshape(N_YL, N_Z, SUB, LANES)


def reduce_grads(message):
    n_xz = N_X * N_Z
    got = exchange(message, Y)
    (send,) = small_call(merge_kernel, [((n_xz, SUB, LANES), BF16)], got)
    got = exchange(send, XZ)
    short_grad, send = small_call(final_kernel, [((SHORT, 64), F32), ((2 * N_Y, 4, LANES), F32)], got)
    return short_grad, exchange(send, SHARE).reshape(TILE, LANES)


def shards(feats, short_filter, medium_filter, doc_ids, counts, plan, cotangent):
    down, up, linked, forward, backward = prepare_call(doc_ids, medium_filter)
    filters = gather_filters(short_filter, counts, plan)
    mixed, gq, gk, gv, message = tile_call(
        counts, plan, feats, filters, down, linked, forward, backward, cotangent
    )
    feats_grad = spread_call((gq, gk, gv), filters, up)
    short_grad, medium_grad = reduce_grads(message)
    return mixed, feats_grad, short_grad, medium_grad


def solution(mesh):
    parts = Mesh(mesh.devices.reshape([size for _, size in PARTS]), ALL)
    in_specs = (P(ALL, None), P(None, ZERO), P(), P(ALL, None), P(ALL), P(ALL), P(ALL, None))
    out_specs = (P(ALL, None), P(ALL, None), P(None, ZERO), P())
    return jax.shard_map(shards, mesh=parts, in_specs=in_specs, out_specs=out_specs, check_vma=False)
```

time: 124 us -> 119 us (0.960)
  blocking collectives: 74.1 us -> 36.6 us
  starting transfers between devices: 13.8 us -> 31.5 us
  waiting for transfers between devices: 7.48 us -> 14.2 us
  Pallas kernels: 23.6 us -> 30.3 us
  local copies, waits for them, and re-layouts: 1.24 us -> 2.51 us
    all_to_all x4 -> x2, blocking collectives: 74.1 us -> 36.6 us  [exchange(): return lax.all_to_all(values, axes, 0, 0, tiled=True)]
    all_to_all x1 -> x3, starting transfers between devices: 13.8 us -> 31.5 us  [exchange(): return lax.all_to_all(values, axes, 0, 0, tiled=True)]
    pallas_call x1 -> x3, Pallas kernels: 18.8 us -> 25.5 us  [the longest x1 12.2 us: tile_call(): pl.pallas_call(tile_kernel, grid=(steps,), in_specs=[SMEM, SMEM] + [block...]
    all_to_all x1 -> x3, waiting for transfers between devices: 7.48 us -> 14.2 us  [exchange(): return lax.all_to_all(values, axes, 0, 0, tiled=True)]
    unnamed x2 -> x5, local copies, waits for them, and re-layouts: 0.61 us -> 1.88 us
  transfers between devices with their start and end apart: 1 -> 3, of which waited for: 1 -> 3; matrix products, arithmetic and copies ran while one was open for 0% -> 0% of each run, Pallas kernels for 0% -> 11%
where the time goes in v2:
time: 119 us; the launch traced here: 118 us
  blocking collectives  36.6 us (31%)
  starting transfers between devices  31.5 us (26%)
  Pallas kernels  30.3 us (25%)
  waiting for transfers between devices  14.2 us (12%)
  local copies, waits for them, and re-layouts  2.51 us (2%)
  between operations  1.98 us (2%)
    all_to_all x2, blocking collectives, exchange(): return lax.all_to_all(values, axes, 0, 0, tiled=True)  36.6 us
    all_to_all x3, starting transfers between devices, exchange(): return lax.all_to_all(values, axes, 0, 0, tiled=True)  31.5 us
    all_to_all x3, waiting for transfers between devices, exchange(): return lax.all_to_all(values, axes, 0, 0, tiled=True)  14.2 us
    pallas_call x1, Pallas kernels, tile_call(): pl.pallas_call(tile_kernel, grid=(steps,), in_specs=[SMEM, SMEM] + [block...  12.2 us
    pallas_call x1, Pallas kernels, prepare_call(): pl.pallas_call(prepare_kernel, grid=(groups // n,), in_specs=[whole((1, T...  7.8 us
    pallas_call x1, Pallas kernels, spread_call(): pl.pallas_call(spread_kernel, grid=(steps,), in_specs=[block()] * 3 + [ta...  5.53 us
    pallas_call x3, Pallas kernels, small_call(): pl.pallas_call(kernel, in_specs=in_specs, out_specs=[pl.BlockSpec(memory_...  4.72 us
  transfers between devices with their start and end apart: 3, of which 3 were waited for; matrix products, arithmetic and copies ran while one was open for 0% of the time, Pallas kernels for 11%

profile of v2, /device:TPU:1, one launch (start us, length us, event | category | flops | bytes accessed | tf_op | source)
XLA Modules:
  0.0 117.8 jit_solution(741917754812453703)
XLA Ops:
  1.9 0.8 pad_select_fusion
  2.7 0.6 broadcast_in_dim.16
  3.3 13.8 %all-to-all-start = ((bf16[16,8,128]{2,1,0:T(8,128)(2,1)}), bf16[16,8,128]{2,1,0:T(8,128)(2,1)S(1)}, u32[]{:S(2)}, u32[]{:S(2)}) async-start(bf16[16,8,128]{2,1,0:T(8,128)(2,1)} %broadcast_in_dim.16), calls=%async_computation | async-start | bytes 65536 | tf_op jit(solution)/shard_map/all_to_all | solution.py:36
  17.1 7.5 %all-to-all-done.got_ref = bf16[16,8,128]{2,1,0:T(8,128)(2,1)S(1)} async-done(((bf16[16,8,128]{2,1,0:T(8,128)(2,1)}), bf16[16,8,128]{2,1,0:T(8,128)(2,1)S(1)}, u32[]{:S(2)}, u32[]{:S(2)}) %all-to-all-start) | async-done | bytes 32800 | tf_op jit(solution)/shard_map/all_to_all | solution.py:36
  24.6 0.0 copy-start.1
  24.6 0.6 copy-done.1
  25.2 1.5 %shard_map.102 = bf16[48,8,128]{2,1,0:T(8,128)(2,1)} custom-call(s32[1]{0:T(128)} %bitcast.x_ref, bf16[16,8,128]{2,1,0:T(8,128)(2,1)} %copy-done.1), custom_call_target="tpu_custom_call" | custom-call | tf_op jit(solution)/shard_map/pallas_call | solution.py:328
  26.7 12.8 %all-to-all-start.1 = ((bf16[48,8,128]{2,1,0:T(8,128)(2,1)}), bf16[48,8,128]{2,1,0:T(8,128)(2,1)S(1)}, u32[]{:S(2)}, u32[]{:S(2)}) async-start(bf16[48,8,128]{2,1,0:T(8,128)(2,1)} %shard_map.102), calls=%async_computation.1 | async-start | bytes 196608 | tf_op jit(solution)/shard_map/all_to_all | solution.py:36
  39.5 7.8 %prepare.1 = (bf16[896,128]{1,0:T(8,128)(2,1)}, bf16[768,128]{1,0:T(8,128)(2,1)}, f32[128,128]{1,0:T(8,128)}, bf16[128,16384]{1,0:T(8,128)(2,1)}, bf16[128,16384]{1,0:T(8,128)(2,1)}) custom-call(s32[1,128]{1,0:T(1,128)} %seg_ref.1, f32[128,128]{1,0:T(8,128)} %medium_ref.1), custom_call_target="tpu_custom_call" | custom-call | tf_op jit(solution)/shard_map/prepare/pallas_call | solution.py:267
  47.3 4.1 %all-to-all-done.1.every_ref = bf16[48,8,128]{2,1,0:T(8,128)(2,1)S(1)} async-done(((bf16[48,8,128]{2,1,0:T(8,128)(2,1)}), bf16[48,8,128]{2,1,0:T(8,128)(2,1)S(1)}, u32[]{:S(2)}, u32[]{:S(2)}) %all-to-all-start.1) | async-done | bytes 98336 | tf_op jit(solution)/shard_map/all_to_all | solution.py:36
  51.3 0.0 copy-start
  51.3 0.6 copy-done
  52.0 12.2 %tile.1 = (bf16[128,2048]{1,0:T(8,128)(2,1)}, bf16[128,2048]{1,0:T(8,128)(2,1)}, bf16[128,2048]{1,0:T(8,128)(2,1)}, bf16[128,2048]{1,0:T(8,128)(2,1)}, bf16[16,56,128]{2,1,0:T(8,128)(2,1)}) custom-call(s32[1]{0:T(128)} %copy.12.count_ref, s32[1]{0:T(128)} %copy.13.plan_ref, bf16[128,6144]{1,0:T(8,128)(2,1)} %fv_ref.1, bf16[128,6144]{1,0:T(8,128)(2,1)} %fv_ref.1, ...), custom_call_target="tpu_custom_call" | custom-call | tf_op jit(solution)/shard_map/tile/pallas_call | solution.py:292
  64.2 17.4 %all_to_all.25.got_ref = bf16[16,56,128]{2,1,0:T(8,128)(2,1)} all-to-all(bf16[16,56,128]{2,1,0:T(8,128)(2,1)} %get-tuple-element.25), channel_id=1, replica_groups=mesh['y_hi'=2,'x_hi'=2,'x_lo'=2,'z'=12,'y_lo'=4,'core'=2] {'y_hi','y_lo'..., dimensions={0} | all-to-all | bytes 458752 | tf_op jit(solution)/shard_map/all_to_all | solution.py:36
  81.6 1.6 %shard_map.103 = bf16[48,8,128]{2,1,0:T(8,128)(2,1)} custom-call(bf16[16,56,128]{2,1,0:T(8,128)(2,1)} %all_to_all.25.got_ref), custom_call_target="tpu_custom_call" | custom-call | tf_op jit(solution)/shard_map/pallas_call | solution.py:328
  83.2 19.2 %all_to_all.26.got_ref = bf16[48,8,128]{2,1,0:T(8,128)(2,1)} all-to-all(bf16[48,8,128]{2,1,0:T(8,128)(2,1)} %shard_map.103), channel_id=1, replica_groups=mesh['y_hi'=2,'x_hi'=2,'x_lo'=2,'z'=12,'y_lo'=4,'core'=2] {'x_hi','x_lo'..., dimensions={0} | all-to-all | bytes 196608 | tf_op jit(solution)/shard_map/all_to_all | solution.py:36
  102.4 1.6 %shard_map.104 = (f32[7,64]{1,0:T(8,128)}, f32[32,4,128]{2,1,0:T(4,128)}) custom-call(bf16[48,8,128]{2,1,0:T(8,128)(2,1)} %all_to_all.26.got_ref), custom_call_target="tpu_custom_call" | custom-call | tf_op jit(solution)/shard_map/pallas_call | solution.py:328
  104.0 5.0 %all-to-all-start.4 = ((f32[32,4,128]{2,1,0:T(4,128)}), f32[32,4,128]{2,1,0:T(4,128)S(1)}, u32[]{:S(2)}, u32[]{:S(2)}) async-start(f32[32,4,128]{2,1,0:T(4,128)} %get-tuple-element.27), calls=%async_computation.4 | async-start | bytes 131072 | tf_op jit(solution)/shard_map/all_to_all | solution.py:36
  109.0 5.5 %spread.1 = bf16[128,6144]{1,0:T(8,128)(2,1)} custom-call(bf16[128,2048]{1,0:T(8,128)(2,1)} %get-tuple-element.21.gq_ref, bf16[128,2048]{1,0:T(8,128)(2,1)} %get-tuple-element.22.gk_ref, bf16[128,2048]{1,0:T(8,128)(2,1)} %get-tuple-element.23.gv_ref, bf16[4,12,8,128]{3,2,1,0:T(8,128)(2,1)} %bitcast.10, bf16[4,12,8,128]{3,2,1,0:T(8,128)(2,1)} %bitcast.11, ...), custom_call_target="tpu_custom_call" | custom-call | tf_op jit(solution)/shard_map/spread/pallas_call | solution.py:313
  114.6 2.6 %all-to-all-done.4 = f32[32,4,128]{2,1,0:T(4,128)S(1)} async-done(((f32[32,4,128]{2,1,0:T(4,128)}), f32[32,4,128]{2,1,0:T(4,128)S(1)}, u32[]{:S(2)}, u32[]{:S(2)}) %all-to-all-start.4) | async-done | bytes 65568 | tf_op jit(solution)/shard_map/all_to_all | solution.py:36
  117.2 0.6 copy.14
  (2 shorter events, 0.0 us)
Async XLA Ops:
  3.3 21.2 %all-to-all-start = ((bf16[16,8,128]{2,1,0:T(8,128)(2,1)}), bf16[16,8,128]{2,1,0:T(8,128)(2,1)S(1)}, u32[]{:S(2)}, u32[]{:S(2)}) async-start(bf16[16,8,128]{2,1,0:T(8,128)(2,1)} %broadcast_in_dim.16), calls=%async_computation | async-start | bytes 65536 | tf_op jit(solution)/shard_map/all_to_all | solution.py:36
  24.6 0.6 copy-start.1
  26.7 24.7 %all-to-all-start.1 = ((bf16[48,8,128]{2,1,0:T(8,128)(2,1)}), bf16[48,8,128]{2,1,0:T(8,128)(2,1)S(1)}, u32[]{:S(2)}, u32[]{:S(2)}) async-start(bf16[48,8,128]{2,1,0:T(8,128)(2,1)} %shard_map.102), calls=%async_computation.1 | async-start | bytes 196608 | tf_op jit(solution)/shard_map/all_to_all | solution.py:36
  51.3 0.6 copy-start
  104.0 13.2 %all-to-all-start.4 = ((f32[32,4,128]{2,1,0:T(4,128)}), f32[32,4,128]{2,1,0:T(4,128)S(1)}, u32[]{:S(2)}, u32[]{:S(2)}) async-start(f32[32,4,128]{2,1,0:T(4,128)} %get-tuple-element.27), calls=%async_computation.4 | async-start | bytes 131072 | tf_op jit(solution)/shard_map/all_to_all | solution.py:36

commit v3 on v2

--- a/solution.py
+++ b/solution.py
@@ -9,7 +9,7 @@
 TILE = 128
 LANES = 128
 WIDTH = 512
-PER_Z = 512 // WIDTH
+PER_STEP = WIDTH // 512
 GSIZE = 16
 SUB = 8
 RANKS = 8
@@ -34,6 +34,17 @@
 
 def exchange(values, axes):
     return lax.all_to_all(values, axes, 0, 0, tiled=True)
+
+
+def first_kernel(count_ref, plan_ref, filter_ref, out_ref, tile_ref):
+    lane = iota((SUB, LANES), 1)
+    row = iota((SUB, LANES), 0)
+    tile_ref[...] = jnp.zeros((SUB, LANES), F32)
+    tile_ref[0:SHORT, 0:64] = filter_ref[...].astype(F32)
+    live = jnp.where(lane == plan_ref[0], count_ref[0].astype(F32), 0.0)
+    tile = jnp.where(row == SHORT, live, tile_ref[...]).astype(BF16)
+    for i in range(out_ref.shape[0]):
+        out_ref[i] = tile
 
 
 def pair_kernel(x_ref, got_ref, out_ref):
@@ -109,9 +120,16 @@
         backward_ref[:, where] = jnp.where(upper, base, 0.0).astype(BF16)
 
 
+def taps_here(every_ref, part, step):
+    tiles = []
+    for h in range(WIDTH // LANES):
+        z = part * (N_Z // 3) + step * PER_STEP + h // N_YL
+        tiles.append(every_ref[(h % N_YL) * N_Z + z].astype(F32))
+    return jnp.concatenate(tiles, 1)
+
+
 def tile_kernel(
-    count_ref, plan_ref, fq_ref, fk_ref, fv_ref, sq_ref, sk_ref, sv_ref,
-    every_ref, down_ref, linked_ref, forward_ref, backward_ref, cot_ref,
+    count_ref, plan_ref, fq_ref, fk_ref, fv_ref, every_ref, down_ref, linked_ref, forward_ref, backward_ref, cot_ref,
     mixed_ref, gq_ref, gk_ref, gv_ref, msg_ref,
     scale_ref, short_ref, med_ref,
 ):
@@ -138,18 +156,18 @@
     living = iota((TILE, WIDTH), 0) < count_ref[0]
     lane_group = iota((TILE, LANES), 1) // GSIZE
 
-    def conv(f_ref, s_ref):
+    def conv(part, f_ref):
         feats = f_ref[...]
-        taps = jnp.concatenate([s_ref[h, 0].astype(F32) for h in range(halves)], 1)
+        taps = taps_here(every_ref, part, step)
         shifted = jnp.dot(down_ref[: (SHORT - 1) * TILE], feats, preferred_element_type=F32)
         total = feats.astype(F32) * taps[0:1]
         for j in range(1, SHORT):
             total = total + shifted[(j - 1) * TILE : j * TILE] * taps[j : j + 1]
         return total, shifted
 
-    query, q_shift = conv(fq_ref, sq_ref)
-    key, k_shift = conv(fk_ref, sk_ref)
-    value, v_shift = conv(fv_ref, sv_ref)
+    query, q_shift = conv(0, fq_ref)
+    key, k_shift = conv(1, fk_ref)
+    value, v_shift = conv(2, fv_ref)
     product = (key * value).astype(BF16)
     flipped = jnp.dot(down_ref[(SHORT - 1) * TILE :], product, preferred_element_type=F32).astype(BF16)
     gout = cot_ref[...].astype(F32) * scale
@@ -191,11 +209,11 @@
             sums.append(jnp.sum(grad * shifted[(j - 1) * TILE : j * TILE], 0, keepdims=True))
         sums.append(jnp.zeros((1, WIDTH), F32))
         sums = jnp.concatenate(sums, 0)
-        z = part * (N_Z // 3) + step // PER_Z
         for h in range(halves):
             tile = sums[:, h * LANES : (h + 1) * LANES]
             other = pltpu.roll(pltpu.roll(tile, 64, 1), 4, 0)
-            short_ref[z * N_YL + lax.rem(step, PER_Z) * halves + h] = jnp.where(keep, tile, other)
+            z = part * (N_Z // 3) + step * PER_STEP + h // N_YL
+            short_ref[z * N_YL + h % N_YL] = jnp.where(keep, tile, other)
 
     taps_grad(0, gout * long_conv, fq_ref, q_shift, gq_ref)
     taps_grad(1, gprod * value, fk_ref, k_shift, gk_ref)
@@ -213,7 +231,7 @@
                     msg_ref[to] = jnp.concatenate(tiles + pieces, 0).astype(BF16)
 
 
-def spread_kernel(gq_ref, gk_ref, gv_ref, sq_ref, sk_ref, sv_ref, up_ref, dfeats_ref, stage_ref, sems):
+def spread_kernel(gq_ref, gk_ref, gv_ref, every_ref, up_ref, dfeats_ref, stage_ref, sems):
     step, steps = pl.program_id(0), pl.num_programs(0)
     width = gq_ref.shape[1]
 
@@ -228,9 +246,9 @@
         for part in range(3):
             store(part, step - 2).wait()
 
-    for part, (g_ref, s_ref) in enumerate(((gq_ref, sq_ref), (gk_ref, sk_ref), (gv_ref, sv_ref))):
+    for part, g_ref in enumerate((gq_ref, gk_ref, gv_ref)):
         grad = g_ref[...]
-        taps = jnp.concatenate([s_ref[h, 0].astype(F32) for h in range(s_ref.shape[0])], 1)
+        taps = taps_here(every_ref, part, step)
         shifted = jnp.dot(up_ref[...], grad, preferred_element_type=F32)
         total = grad.astype(F32) * taps[0:1]
         for j in range(1, SHORT):
@@ -253,11 +271,8 @@
     return pl.BlockSpec((rows, WIDTH), lambda i: (0, part * steps + i))
 
 
-def taps_block(part):
-    return pl.BlockSpec((WIDTH // LANES, 1, SUB, LANES), lambda i: (lax.rem(i, PER_Z), part * (N_Z // 3) + i // PER_Z, 0, 0))
-
-
 SMEM = pl.BlockSpec(memory_space=pltpu.SMEM)
+VMEM = pl.BlockSpec(memory_space=pltpu.VMEM)
 
 
 def prepare_call(doc_ids, medium):
@@ -284,7 +299,6 @@
 def tile_call(count, plan, feats, filters, down, linked, forward, backward, cotangent):
     width = cotangent.shape[1]
     steps = width // WIDTH
-    every = filters.reshape(N_YL * N_Z, SUB, LANES)
     toeplitz = pl.BlockSpec((TILE, forward.shape[1] // steps), lambda i: (0, i))
     message = (N_Y, 4 * N_Z + SUB, LANES)
     vmem = pltpu.VMEM
@@ -294,17 +308,16 @@
         grid=(steps,),
         in_specs=[SMEM, SMEM]
         + [block(TILE, p, steps) for p in range(3)]
-        + [taps_block(p) for p in range(3)]
-        + [whole(every.shape), whole(down.shape), whole(linked.shape), toeplitz, toeplitz, block()],
-        out_specs=[block(), block(), block(), block(), whole(message)],
-        out_shape=[part, part, part, part, jax.ShapeDtypeStruct(message, BF16)],
+        + [VMEM, whole(down.shape), whole(linked.shape), toeplitz, toeplitz, block()],
+        out_specs=[block(), block(), block(), block(), VMEM],
+        out_shape=[part, part, part, part, pltpu.VMEM(message, BF16)],
         scratch_shapes=[
             vmem((TILE, TILE), F32),
             vmem((N_Z * N_YL, SUB, LANES), F32),
             vmem((forward.shape[1] // TILE // SUB, SUB, TILE), F32),
         ],
         name="tile",
-    )(count, plan, feats, feats, feats, filters, filters, filters, every, down, linked, forward, backward, cotangent)
+    )(count, plan, feats, feats, feats, filters, down, linked, forward, backward, cotangent)
 
 
 def spread_call(grads, filters, up):
@@ -313,45 +326,48 @@
     return pl.pallas_call(
         spread_kernel,
         grid=(steps,),
-        in_specs=[block()] * 3 + [taps_block(p) for p in range(3)] + [whole(up.shape)],
+        in_specs=[block()] * 3 + [VMEM, whole(up.shape)],
         out_specs=pl.BlockSpec(memory_space=pl.ANY),
         out_shape=jax.ShapeDtypeStruct((TILE, 3 * width), BF16),
         scratch_shapes=[pltpu.VMEM((2, 3, TILE, WIDTH), BF16), pltpu.SemaphoreType.DMA((2, 3))],
         name="spread",
-    )(*grads, filters, filters, filters, up)
-
-
-def small_call(kernel, outs, *operands):
+    )(*grads, filters, up)
+
+
+def small_call(kernel, outs, *operands, scratch=()):
     in_specs = [
         pl.BlockSpec(memory_space=pltpu.SMEM if x.dtype == jnp.int32 else pltpu.VMEM) for x in operands
+    ]
+    operands = [
+        x if x.dtype == jnp.int32 else pltpu.with_memory_space_constraint(x, pltpu.VMEM) for x in operands
     ]
     return pl.pallas_call(
         kernel,
         in_specs=in_specs,
         out_specs=[pl.BlockSpec(memory_space=pltpu.VMEM)] * len(outs),
-        out_shape=[jax.ShapeDtypeStruct(*o) for o in outs],
+        out_shape=[pltpu.VMEM(*o) if keep else jax.ShapeDtypeStruct(*o) for keep, *o in outs],
+        scratch_shapes=scratch,
     )(*operands)
 
 
 def gather_filters(short_filter, counts, plan):
     n_xz = N_X * N_Z
-    lane = iota((SUB, LANES), 1)
-    row = iota((SUB, LANES), 0)
-    padded = jnp.pad(short_filter, ((0, SUB - SHORT), (0, LANES - short_filter.shape[1])))
-    member = jnp.where(lane == plan[0], counts[0], 0).astype(BF16)
-    tile = jnp.where(row == SHORT, member, padded)
-    got = exchange(jnp.broadcast_to(tile[None], (N_Y, SUB, LANES)), Y)
+    (send,) = small_call(
+        first_kernel, [(False, (N_Y, SUB, LANES), BF16)], counts, plan, short_filter,
+        scratch=[pltpu.VMEM((SUB, LANES), F32)],
+    )
+    got = exchange(send, Y)
     where = lax.axis_index(X).astype(jnp.int32).reshape(1)
-    (send,) = small_call(pair_kernel, [((n_xz, SUB, LANES), BF16)], where, got)
-    return exchange(send, XZ).reshape(N_YL, N_Z, SUB, LANES)
+    (send,) = small_call(pair_kernel, [(True, (n_xz, SUB, LANES), BF16)], where, got)
+    return pltpu.with_memory_space_constraint(exchange(send, XZ), pltpu.VMEM)
 
 
 def reduce_grads(message):
     n_xz = N_X * N_Z
     got = exchange(message, Y)
-    (send,) = small_call(merge_kernel, [((n_xz, SUB, LANES), BF16)], got)
+    (send,) = small_call(merge_kernel, [(True, (n_xz, SUB, LANES), BF16)], got)
     got = exchange(send, XZ)
-    short_grad, send = small_call(final_kernel, [((SHORT, 64), F32), ((2 * N_Y, 4, LANES), F32)], got)
+    short_grad, send = small_call(final_kernel, [(False, (SHORT, 64), F32), (True, (2 * N_Y, 4, LANES), F32)], got)
     return short_grad, exchange(send, SHARE).reshape(TILE, LANES)
 
 

time: 119 us -> 111 us (0.933)
  Pallas kernels: 30.3 us -> 27.1 us
  blocking collectives: 36.6 us -> 34.5 us
  local copies, waits for them, and re-layouts: 2.51 us -> 1.3 us
    pallas_call x3 -> x4, Pallas kernels: 4.72 us -> 2.12 us  [small_call(): pl.pallas_call(kernel, in_specs=in_specs, out_specs=[pl.BlockSpec(memory_...]
    all_to_all x2, blocking collectives: 36.6 us -> 34.5 us  [exchange(): return lax.all_to_all(values, axes, 0, 0, tiled=True)]
  transfers between devices with their start and end apart: 3 -> 3, of which waited for: 3 -> 3; matrix products, arithmetic and copies ran while one was open for 0% -> 0% of each run, Pallas kernels for 11% -> 12%
where the time goes in v3:
time: 111 us
  blocking collectives  34.5 us (31%)
  starting transfers between devices  31.5 us (28%)
  Pallas kernels  27.1 us (24%)
  waiting for transfers between devices  14.5 us (13%)
  between operations  1.96 us (2%)
  local copies, waits for them, and re-layouts  1.3 us (1%)
    all_to_all x2, blocking collectives, exchange(): return lax.all_to_all(values, axes, 0, 0, tiled=True)  34.5 us
    all_to_all x3, starting transfers between devices, exchange(): return lax.all_to_all(values, axes, 0, 0, tiled=True)  31.5 us
    all_to_all x3, waiting for transfers between devices, exchange(): return lax.all_to_all(values, axes, 0, 0, tiled=True)  14.5 us
    pallas_call x1, Pallas kernels, tile_call(): pl.pallas_call(tile_kernel, grid=(steps,), in_specs=[SMEM, SMEM] + [block...  12 us
    pallas_call x1, Pallas kernels, prepare_call(): pl.pallas_call(prepare_kernel, grid=(groups // n,), in_specs=[whole((1, T...  7.57 us
    pallas_call x1, Pallas kernels, spread_call(): pl.pallas_call(spread_kernel, grid=(steps,), in_specs=[block()] * 3 + [VM...  5.4 us
  transfers between devices with their start and end apart: 3, of which 3 were waited for; matrix products, arithmetic and copies ran while one was open for 0% of the time, Pallas kernels for 12%

profile of v3, /device:TPU:1, one launch (start us, length us, event | category | flops | bytes accessed | tf_op | source)
XLA Modules:
  0.0 110.9 jit_solution(12210555702801284072)
XLA Ops:
  1.9 0.0 copy-start
  1.9 0.7 copy-done
  2.6 0.6 shard_map.102
  3.2 13.8 %all-to-all-start = ((bf16[16,8,128]{2,1,0:T(8,128)(2,1)}), bf16[16,8,128]{2,1,0:T(8,128)(2,1)S(1)}, u32[]{:S(2)}, u32[]{:S(2)}) async-start(bf16[16,8,128]{2,1,0:T(8,128)(2,1)} %shard_map.102), calls=%async_computation | async-start | bytes 65536 | tf_op jit(solution)/shard_map/all_to_all | solution.py:36
  17.0 7.5 %all-to-all-done.got_ref = bf16[16,8,128]{2,1,0:T(8,128)(2,1)S(1)} async-done(((bf16[16,8,128]{2,1,0:T(8,128)(2,1)}), bf16[16,8,128]{2,1,0:T(8,128)(2,1)S(1)}, u32[]{:S(2)}, u32[]{:S(2)}) %all-to-all-start) | async-done | bytes 32800 | tf_op jit(solution)/shard_map/all_to_all | solution.py:36
  24.5 0.7 shard_map.103
  25.2 12.8 %all-to-all-start.1 = ((bf16[48,8,128]{2,1,0:T(8,128)(2,1)}), bf16[48,8,128]{2,1,0:T(8,128)(2,1)S(1)}, u32[]{:S(2)}, u32[]{:S(2)}) async-start(bf16[48,8,128]{2,1,0:T(8,128)(2,1)} %shard_map.103), calls=%async_computation.1 | async-start | bytes 196608 | tf_op jit(solution)/shard_map/all_to_all | solution.py:36
  38.0 7.6 %prepare.1 = (bf16[896,128]{1,0:T(8,128)(2,1)}, bf16[768,128]{1,0:T(8,128)(2,1)}, f32[128,128]{1,0:T(8,128)}, bf16[128,16384]{1,0:T(8,128)(2,1)}, bf16[128,16384]{1,0:T(8,128)(2,1)}) custom-call(s32[1,128]{1,0:T(1,128)} %seg_ref.1, f32[128,128]{1,0:T(8,128)} %medium_ref.1), custom_call_target="tpu_custom_call" | custom-call | tf_op jit(solution)/shard_map/prepare/pallas_call | solution.py:282
  45.6 4.3 %all-to-all-done.1.every_ref = bf16[48,8,128]{2,1,0:T(8,128)(2,1)S(1)} async-done(((bf16[48,8,128]{2,1,0:T(8,128)(2,1)}), bf16[48,8,128]{2,1,0:T(8,128)(2,1)S(1)}, u32[]{:S(2)}, u32[]{:S(2)}) %all-to-all-start.1) | async-done | bytes 98336 | tf_op jit(solution)/shard_map/all_to_all | solution.py:36
  49.9 12.0 %tile.1 = (bf16[128,2048]{1,0:T(8,128)(2,1)}, bf16[128,2048]{1,0:T(8,128)(2,1)}, bf16[128,2048]{1,0:T(8,128)(2,1)}, bf16[128,2048]{1,0:T(8,128)(2,1)}, bf16[16,56,128]{2,1,0:T(8,128)(2,1)S(1)}) custom-call(s32[1]{0:T(128)S(6)} %copy.12.count_ref, s32[1]{0:T(128)S(6)} %copy.13.plan_ref, bf16[128,6144]{1,0:T(8,128)(2,1)} %fv_ref.1, bf16[128,6144]{1,0:T(8,128)(2,1)} %fv_ref.1, ...), custom_call_target="tpu_custom_call" | custom-call | tf_op jit(solution)/shard_map/tile/pallas_call | solution.py:306
  61.8 15.8 %all_to_all.25.got_ref = bf16[16,56,128]{2,1,0:T(8,128)(2,1)S(1)} all-to-all(bf16[16,56,128]{2,1,0:T(8,128)(2,1)S(1)} %get-tuple-element.25), channel_id=1, replica_groups=mesh['y_hi'=2,'x_hi'=2,'x_lo'=2,'z'=12,'y_lo'=4,'core'=2] {'y_hi','y_lo'..., dimensions={0} | all-to-all | bytes 458752 | tf_op jit(solution)/shard_map/all_to_all | solution.py:36
  77.7 18.6 %all_to_all.26.got_ref = bf16[48,8,128]{2,1,0:T(8,128)(2,1)S(1)} all-to-all(bf16[48,8,128]{2,1,0:T(8,128)(2,1)S(1)} %shard_map.104), channel_id=1, replica_groups=mesh['y_hi'=2,'x_hi'=2,'x_lo'=2,'z'=12,'y_lo'=4,'core'=2] {'x_hi','x_lo'..., dimensions={0} | all-to-all | bytes 196608 | tf_op jit(solution)/shard_map/all_to_all | solution.py:36
  96.3 0.7 shard_map.105
  97.0 5.0 %all-to-all-start.4 = ((f32[32,4,128]{2,1,0:T(4,128)}), f32[32,4,128]{2,1,0:T(4,128)S(1)}, u32[]{:S(2)}, u32[]{:S(2)}) async-start(f32[32,4,128]{2,1,0:T(4,128)} %get-tuple-element.27), calls=%async_computation.4 | async-start | bytes 131072 | tf_op jit(solution)/shard_map/all_to_all | solution.py:36
  102.1 5.4 %spread.1 = bf16[128,6144]{1,0:T(8,128)(2,1)} custom-call(bf16[128,2048]{1,0:T(8,128)(2,1)} %get-tuple-element.21.gq_ref, bf16[128,2048]{1,0:T(8,128)(2,1)} %get-tuple-element.22.gk_ref, bf16[128,2048]{1,0:T(8,128)(2,1)} %get-tuple-element.23.gv_ref, bf16[48,8,128]{2,1,0:T(8,128)(2,1)S(1)} %all-to-all-done.1.every_ref, bf16[768,128]{1,0:T(8,128)(2,1)} %get-tuple-element.24.up_ref), custom_call_target="tpu_custom_call" | custom-call | tf_op jit(solution)/shard_map/spread/pallas_call | solution.py:326
  107.5 2.8 %all-to-all-done.4 = f32[32,4,128]{2,1,0:T(4,128)S(1)} async-done(((f32[32,4,128]{2,1,0:T(4,128)}), f32[32,4,128]{2,1,0:T(4,128)S(1)}, u32[]{:S(2)}, u32[]{:S(2)}) %all-to-all-start.4) | async-done | bytes 65568 | tf_op jit(solution)/shard_map/all_to_all | solution.py:36
  110.2 0.6 copy.14
  (1 shorter events, 0.0 us)
Async XLA Ops:
  1.9 0.7 copy-start
  3.2 21.2 %all-to-all-start = ((bf16[16,8,128]{2,1,0:T(8,128)(2,1)}), bf16[16,8,128]{2,1,0:T(8,128)(2,1)S(1)}, u32[]{:S(2)}, u32[]{:S(2)}) async-start(bf16[16,8,128]{2,1,0:T(8,128)(2,1)} %shard_map.102), calls=%async_computation | async-start | bytes 65536 | tf_op jit(solution)/shard_map/all_to_all | solution.py:36
  25.2 24.7 %all-to-all-start.1 = ((bf16[48,8,128]{2,1,0:T(8,128)(2,1)}), bf16[48,8,128]{2,1,0:T(8,128)(2,1)S(1)}, u32[]{:S(2)}, u32[]{:S(2)}) async-start(bf16[48,8,128]{2,1,0:T(8,128)(2,1)} %shard_map.103), calls=%async_computation.1 | async-start | bytes 196608 | tf_op jit(solution)/shard_map/all_to_all | solution.py:36
  97.0 13.2 %all-to-all-start.4 = ((f32[32,4,128]{2,1,0:T(4,128)}), f32[32,4,128]{2,1,0:T(4,128)S(1)}, u32[]{:S(2)}, u32[]{:S(2)}) async-start(f32[32,4,128]{2,1,0:T(4,128)} %get-tuple-element.27), calls=%async_computation.4 | async-start | bytes 131072 | tf_op jit(solution)/shard_map/all_to_all | solution.py:36

commit v4 on v3

--- a/solution.py
+++ b/solution.py
@@ -283,11 +283,11 @@
         prepare_kernel,
         grid=(groups // n,),
         in_specs=[whole((1, TILE)), whole(medium.shape)],
-        out_specs=[whole((SHORT * TILE, TILE)), whole(((SHORT - 1) * TILE, TILE)), whole((TILE, TILE)), rows, rows],
+        out_specs=[VMEM, whole(((SHORT - 1) * TILE, TILE)), VMEM, rows, rows],
         out_shape=[
-            jax.ShapeDtypeStruct((SHORT * TILE, TILE), BF16),
+            pltpu.VMEM((SHORT * TILE, TILE), BF16),
             jax.ShapeDtypeStruct(((SHORT - 1) * TILE, TILE), BF16),
-            jax.ShapeDtypeStruct((TILE, TILE), F32),
+            pltpu.VMEM((TILE, TILE), F32),
             jax.ShapeDtypeStruct((TILE, groups * TILE), BF16),
             jax.ShapeDtypeStruct((TILE, groups * TILE), BF16),
         ],
@@ -308,7 +308,7 @@
         grid=(steps,),
         in_specs=[SMEM, SMEM]
         + [block(TILE, p, steps) for p in range(3)]
-        + [VMEM, whole(down.shape), whole(linked.shape), toeplitz, toeplitz, block()],
+        + [VMEM, VMEM, VMEM, toeplitz, toeplitz, block()],
         out_specs=[block(), block(), block(), block(), VMEM],
         out_shape=[part, part, part, part, pltpu.VMEM(message, BF16)],
         scratch_shapes=[

time: 111 us -> 113 us (1.018)
  local copies, waits for them, and re-layouts: 1.3 us -> 2.62 us
  blocking collectives: 34.5 us -> 35.7 us
  waiting for transfers between devices: 14.5 us -> 13.3 us
    unnamed x3 -> x7, local copies, waits for them, and re-layouts: 1.3 us -> 2.62 us
    all_to_all x3, waiting for transfers between devices: 14.5 us -> 13.3 us  [exchange(): return lax.all_to_all(values, axes, 0, 0, tiled=True)]
    all_to_all x2, blocking collectives: 34.5 us -> 35.7 us  [exchange(): return lax.all_to_all(values, axes, 0, 0, tiled=True)]
where the time goes in v4:
time: 113 us; the launch traced here: 112 us
  blocking collectives  35.7 us (32%)
  starting transfers between devices  31.5 us (28%)
  Pallas kernels  27 us (24%)
  waiting for transfers between devices  13.3 us (12%)
  local copies, waits for them, and re-layouts  2.62 us (2%)
  between operations  1.97 us (2%)
    all_to_all x2, blocking collectives, exchange(): return lax.all_to_all(values, axes, 0, 0, tiled=True)  35.7 us
    all_to_all x3, starting transfers between devices, exchange(): return lax.all_to_all(values, axes, 0, 0, tiled=True)  31.5 us
    all_to_all x3, waiting for transfers between devices, exchange(): return lax.all_to_all(values, axes, 0, 0, tiled=True)  13.3 us
    pallas_call x1, Pallas kernels, tile_call(): pl.pallas_call(tile_kernel, grid=(steps,), in_specs=[SMEM, SMEM] + [block...  12 us
    pallas_call x1, Pallas kernels, prepare_call(): pl.pallas_call(prepare_kernel, grid=(groups // n,), in_specs=[whole((1, T...  7.52 us
    pallas_call x1, Pallas kernels, spread_call(): pl.pallas_call(spread_kernel, grid=(steps,), in_specs=[block()] * 3 + [VM...  5.4 us
    unnamed x7, local copies, waits for them, and re-layouts  2.62 us
  transfers between devices with their start and end apart: 3, of which 3 were waited for; matrix products, arithmetic and copies ran while one was open for 0% of the time, Pallas kernels for 12%

profile of v4, /device:TPU:1, one launch (start us, length us, event | category | flops | bytes accessed | tf_op | source)
XLA Modules:
  0.0 112.1 jit_solution(4914552037211221794)
XLA Ops:
  1.9 0.0 copy-start.2
  1.9 0.7 copy-done.2
  2.6 0.6 shard_map.102
  3.2 13.8 %all-to-all-start = ((bf16[16,8,128]{2,1,0:T(8,128)(2,1)}), bf16[16,8,128]{2,1,0:T(8,128)(2,1)S(1)}, u32[]{:S(2)}, u32[]{:S(2)}) async-start(bf16[16,8,128]{2,1,0:T(8,128)(2,1)} %shard_map.102), calls=%async_computation | async-start | bytes 65536 | tf_op jit(solution)/shard_map/all_to_all | solution.py:36
  17.0 7.5 %all-to-all-done.got_ref = bf16[16,8,128]{2,1,0:T(8,128)(2,1)S(1)} async-done(((bf16[16,8,128]{2,1,0:T(8,128)(2,1)}), bf16[16,8,128]{2,1,0:T(8,128)(2,1)S(1)}, u32[]{:S(2)}, u32[]{:S(2)}) %all-to-all-start) | async-done | bytes 32800 | tf_op jit(solution)/shard_map/all_to_all | solution.py:36
  24.5 0.7 shard_map.103
  25.2 12.8 %all-to-all-start.1 = ((bf16[48,8,128]{2,1,0:T(8,128)(2,1)}), bf16[48,8,128]{2,1,0:T(8,128)(2,1)S(1)}, u32[]{:S(2)}, u32[]{:S(2)}) async-start(bf16[48,8,128]{2,1,0:T(8,128)(2,1)} %shard_map.103), calls=%async_computation.1 | async-start | bytes 196608 | tf_op jit(solution)/shard_map/all_to_all | solution.py:36
  38.0 7.5 %prepare.1 = (bf16[896,128]{1,0:T(8,128)(2,1)S(1)}, bf16[768,128]{1,0:T(8,128)(2,1)}, f32[128,128]{1,0:T(8,128)S(1)}, bf16[128,16384]{1,0:T(8,128)(2,1)}, bf16[128,16384]{1,0:T(8,128)(2,1)}) custom-call(s32[1,128]{1,0:T(1,128)} %seg_ref.1, f32[128,128]{1,0:T(8,128)} %medium_ref.1), custom_call_target="tpu_custom_call" | custom-call | tf_op jit(solution)/shard_map/prepare/pallas_call | solution.py:282
  45.5 0.0 copy-start
  45.5 0.7 copy-done
  46.2 0.0 copy-start.1
  46.2 0.6 copy-done.1
  46.8 3.0 %all-to-all-done.1.every_ref = bf16[48,8,128]{2,1,0:T(8,128)(2,1)S(1)} async-done(((bf16[48,8,128]{2,1,0:T(8,128)(2,1)}), bf16[48,8,128]{2,1,0:T(8,128)(2,1)S(1)}, u32[]{:S(2)}, u32[]{:S(2)}) %all-to-all-start.1) | async-done | bytes 98336 | tf_op jit(solution)/shard_map/all_to_all | solution.py:36
  49.9 12.0 %tile.1 = (bf16[128,2048]{1,0:T(8,128)(2,1)}, bf16[128,2048]{1,0:T(8,128)(2,1)}, bf16[128,2048]{1,0:T(8,128)(2,1)}, bf16[128,2048]{1,0:T(8,128)(2,1)}, bf16[16,56,128]{2,1,0:T(8,128)(2,1)S(1)}) custom-call(s32[1]{0:T(128)S(6)} %copy.12.count_ref, s32[1]{0:T(128)S(6)} %copy.13.plan_ref, bf16[128,6144]{1,0:T(8,128)(2,1)} %fv_ref.1, bf16[128,6144]{1,0:T(8,128)(2,1)} %fv_ref.1, ...), custom_call_target="tpu_custom_call" | custom-call | tf_op jit(solution)/shard_map/tile/pallas_call | solution.py:306
  61.8 15.8 %all_to_all.25.got_ref = bf16[16,56,128]{2,1,0:T(8,128)(2,1)S(1)} all-to-all(bf16[16,56,128]{2,1,0:T(8,128)(2,1)S(1)} %get-tuple-element.25), channel_id=1, replica_groups=mesh['y_hi'=2,'x_hi'=2,'x_lo'=2,'z'=12,'y_lo'=4,'core'=2] {'y_hi','y_lo'..., dimensions={0} | all-to-all | bytes 458752 | tf_op jit(solution)/shard_map/all_to_all | solution.py:36
  77.7 19.9 %all_to_all.26.got_ref = bf16[48,8,128]{2,1,0:T(8,128)(2,1)S(1)} all-to-all(bf16[48,8,128]{2,1,0:T(8,128)(2,1)S(1)} %shard_map.104), channel_id=1, replica_groups=mesh['y_hi'=2,'x_hi'=2,'x_lo'=2,'z'=12,'y_lo'=4,'core'=2] {'x_hi','x_lo'..., dimensions={0} | all-to-all | bytes 196608 | tf_op jit(solution)/shard_map/all_to_all | solution.py:36
  97.6 0.7 shard_map.105
  98.3 5.0 %all-to-all-start.4 = ((f32[32,4,128]{2,1,0:T(4,128)}), f32[32,4,128]{2,1,0:T(4,128)S(1)}, u32[]{:S(2)}, u32[]{:S(2)}) async-start(f32[32,4,128]{2,1,0:T(4,128)} %get-tuple-element.27), calls=%async_computation.4 | async-start | bytes 131072 | tf_op jit(solution)/shard_map/all_to_all | solution.py:36
  103.3 5.4 %spread.1 = bf16[128,6144]{1,0:T(8,128)(2,1)} custom-call(bf16[128,2048]{1,0:T(8,128)(2,1)} %get-tuple-element.21.gq_ref, bf16[128,2048]{1,0:T(8,128)(2,1)} %get-tuple-element.22.gk_ref, bf16[128,2048]{1,0:T(8,128)(2,1)} %get-tuple-element.23.gv_ref, bf16[48,8,128]{2,1,0:T(8,128)(2,1)S(1)} %all-to-all-done.1.every_ref, bf16[768,128]{1,0:T(8,128)(2,1)} %get-tuple-element.24.up_ref), custom_call_target="tpu_custom_call" | custom-call | tf_op jit(solution)/shard_map/spread/pallas_call | solution.py:326
  108.7 2.8 %all-to-all-done.4 = f32[32,4,128]{2,1,0:T(4,128)S(1)} async-done(((f32[32,4,128]{2,1,0:T(4,128)}), f32[32,4,128]{2,1,0:T(4,128)S(1)}, u32[]{:S(2)}, u32[]{:S(2)}) %all-to-all-start.4) | async-done | bytes 65568 | tf_op jit(solution)/shard_map/all_to_all | solution.py:36
  111.5 0.6 copy.14
  (1 shorter events, 0.0 us)
Async XLA Ops:
  1.9 0.7 copy-start.2
  3.2 21.2 %all-to-all-start = ((bf16[16,8,128]{2,1,0:T(8,128)(2,1)}), bf16[16,8,128]{2,1,0:T(8,128)(2,1)S(1)}, u32[]{:S(2)}, u32[]{:S(2)}) async-start(bf16[16,8,128]{2,1,0:T(8,128)(2,1)} %shard_map.102), calls=%async_computation | async-start | bytes 65536 | tf_op jit(solution)/shard_map/all_to_all | solution.py:36
  25.2 24.7 %all-to-all-start.1 = ((bf16[48,8,128]{2,1,0:T(8,128)(2,1)}), bf16[48,8,128]{2,1,0:T(8,128)(2,1)S(1)}, u32[]{:S(2)}, u32[]{:S(2)}) async-start(bf16[48,8,128]{2,1,0:T(8,128)(2,1)} %shard_map.103), calls=%async_computation.1 | async-start | bytes 196608 | tf_op jit(solution)/shard_map/all_to_all | solution.py:36
  45.5 0.7 copy-start
  46.2 0.6 copy-start.1
  98.3 13.2 %all-to-all-start.4 = ((f32[32,4,128]{2,1,0:T(4,128)}), f32[32,4,128]{2,1,0:T(4,128)S(1)}, u32[]{:S(2)}, u32[]{:S(2)}) async-start(f32[32,4,128]{2,1,0:T(4,128)} %get-tuple-element.27), calls=%async_computation.4 | async-start | bytes 131072 | tf_op jit(solution)/shard_map/all_to_all | solution.py:36
